TPU v7x, 32 devices: a whole 2x2x4 slice. The times are simulated.
32 devices in a mesh: ctx: 8 (over z, x), tp: 4 (over y, core).
Axes of the slice: x: 2, y: 2, z: 4, core: 2. Of those that a mesh axis runs over, the one named last changes fastest.
Arguments:
- features: bfloat16 [2048, 3, 4096], P('ctx', None, 'tp'), may hold values from -6 to 6
- short_filter: float32 [3, 3, 4096], P(None, None, 'tp'), may hold values from -3 to 3
- log_decay: float32 [16, 4096], P(None, 'tp'), may hold values from 0.00012207031 to 0.0333333333
- residue: float32 [16, 4096], P(None, 'tp'), may hold values from -0.52 to 0.52
- residual: bfloat16 [2048, 4096], P('ctx', 'tp'), may hold values from -6 to 6
- out_weight: bfloat16 [4096, 4096], P(('ctx', 'tp')), may hold values from -0.09375 to 0.09375
Outputs:
- mixed: bfloat16 [2048, 4096], P('ctx', 'tp')
All inputs are finite; a program needn't handle non-finite values.
Results may differ from a plain program's by a relative error of at most 0.0048.
Values may be sent and summed in bfloat16 or wider, within the bound.
No kernel may reach another device: no remote copies, remote signals or barrier semaphores. Data moves between devices by JAX's collectives and lax.ppermute only.
A program may use at most 128 MiB of HBM per device.

v0:
```python
import functools

import jax
import jax.numpy as jnp
from jax import lax
from jax.experimental import pallas as pl
from jax.experimental.pallas import tpu as pltpu
from jax.sharding import PartitionSpec as P


LANES = 128
CHUNKS = 2
UNROLL = 16
Z_CUT, X_CUT = 6, 4
SEGS = 8


def row(ref_value, n):
    return jnp.broadcast_to(ref_value[n : n + 1, :], (SEGS, ref_value.shape[1]))


def shifted(value, halo_row):
    lane_row = lax.broadcasted_iota(jnp.int32, value.shape, 0)
    return jnp.where(lane_row == 0, halo_row, pltpu.roll(value, 1, 0))


def history(tokens, halo, stream, lanes, seg_len, filter_len):
    rim = halo[stream, :, lanes].astype(jnp.float32)
    past = []
    for back in range(1, filter_len):
        last = tokens[pl.ds(seg_len - back, SEGS, stride=seg_len), :]
        past.append(shifted(last, rim[filter_len - 1 - back : filter_len - back, :]))
    return past


def taps_of(taps, stream, lanes, filter_len):
    values = taps[stream, :, lanes]
    return [row(values, j) for j in range(filter_len)]


def filter_step(now, past, taps):
    total = taps[0] * now
    for tap, old in zip(taps[1:], past):
        total = total + tap * old
    return total, [now] + past[:-1]


def scan_kernel(
    seg_len, feats, halo, taps, decay, driven, end, before, k_rows, v_rows
):
    modes, channels = decay.shape
    filter_len = taps.shape[1]
    seg = lax.broadcasted_iota(jnp.int32, (SEGS, LANES), 0)

    def one_group(group, _):
        lanes = pl.ds(pl.multiple_of(group * LANES, LANES), LANES)
        rate = decay[:, lanes]
        per_token = jnp.exp(-rate)
        step = [row(per_token, n) for n in range(modes)]
        k_rows[...] = feats[1, :, lanes].astype(jnp.float32)
        v_rows[...] = feats[2, :, lanes].astype(jnp.float32)
        k_taps = taps_of(taps, 1, lanes, filter_len)
        v_taps = taps_of(taps, 2, lanes, filter_len)

        def one_token(i, carry):
            states, k_past, v_past = carry
            at = pl.ds(i, SEGS, stride=seg_len)
            k, k_past = filter_step(k_rows[at, :], k_past, k_taps)
            v, v_past = filter_step(v_rows[at, :], v_past, v_taps)
            drive = k * v
            driven[i, :, lanes] = drive
            states = [a * s + drive for a, s in zip(step, states)]
            return states, k_past, v_past

        zero = jnp.zeros((SEGS, LANES), jnp.float32)
        states, _, _ = lax.fori_loop(
            0,
            seg_len,
            one_token,
            (
                [zero] * modes,
                history(k_rows, halo, 1, lanes, seg_len, filter_len),
                history(v_rows, halo, 2, lanes, seg_len, filter_len),
            ),
            unroll=UNROLL,
        )
        hop = 1
        while hop < SEGS:
            weight = jnp.exp(-rate * float(seg_len * hop))
            states = [
                s + row(weight, n) * jnp.where(seg >= hop, pltpu.roll(s, hop, 0), 0.0)
                for n, s in enumerate(states)
            ]
            hop *= 2
        for n, s in enumerate(states):
            end[n : n + 1, lanes] = s[SEGS - 1 :, :]
            before[n, :, lanes] = jnp.where(seg >= 1, pltpu.roll(s, 1, 0), 0.0)
        return 0

    lax.fori_loop(0, channels // LANES, one_group, 0)


def local_kernel(
    seg_len, feats, halo, taps, decay, residue, driven, before, gate, local, q_rows
):
    modes, channels = decay.shape
    filter_len = taps.shape[1]

    def one_group(group, _):
        lanes = pl.ds(pl.multiple_of(group * LANES, LANES), LANES)
        per_token = jnp.exp(-decay[:, lanes])
        weights = residue[:, lanes]
        q_rows[...] = feats[0, :, lanes].astype(jnp.float32)
        step = [row(per_token, n) for n in range(modes)]
        gain = [row(weights, n) for n in range(modes)]
        q_taps = taps_of(taps, 0, lanes, filter_len)

        def one_token(i, carry):
            states, q_past = carry
            at = pl.ds(i, SEGS, stride=seg_len)
            now, q_past = filter_step(q_rows[at, :], q_past, q_taps)
            gate[i, :, lanes] = now
            drive = driven[i, :, lanes]
            states = [a * s + drive for a, s in zip(step, states)]
            local[i, :, lanes] = tree_sum([r * s for r, s in zip(gain, states)])
            return states, q_past

        lax.fori_loop(
            0,
            seg_len,
            one_token,
            (
                [before[n, :, lanes] for n in range(modes)],
                history(q_rows, halo, 0, lanes, seg_len, filter_len),
            ),
            unroll=UNROLL,
        )
        return 0

    lax.fori_loop(0, channels // LANES, one_group, 0)


def tree_sum(terms):
    while len(terms) > 1:
        terms = [a + b for a, b in zip(terms[::2], terms[1::2])] + terms[len(terms) & ~1 :]
    return terms[0]


def output_kernel(seg_len, parts, flags, decay, residue, gate, local, incoming, *refs):
    outs, rows = refs[:parts], refs[parts]
    modes, channels = decay.shape
    seg = lax.broadcasted_iota(jnp.int32, (SEGS, LANES), 0).astype(jnp.float32)

    def one_group(group, _):
        lanes = pl.ds(pl.multiple_of(group * LANES, LANES), LANES)
        rate = decay[:, lanes]
        per_token = jnp.exp(-rate)
        entering = residue[:, lanes] * incoming[:, lanes]
        step = [row(per_token, n) for n in range(modes)]
        since = seg * float(seg_len) + 1.0
        terms = [jnp.exp(-row(rate, n) * since) * row(entering, n) for n in range(modes)]

        def one_token(i, terms):
            total = local[i, :, lanes] + tree_sum(terms)
            rows[pl.ds(i, SEGS, stride=seg_len), :] = gate[i, :, lanes] * total
            return [a * term for a, term in zip(step, terms)]

        lax.fori_loop(0, seg_len, one_token, terms, unroll=UNROLL)
        place = pl.ds(pl.multiple_of((group // parts) * LANES, LANES), LANES)
        value = rows[...].astype(jnp.bfloat16)
        turned = jnp.bitwise_xor(lax.rem(group, parts), flags[0] if parts > 1 else 0)
        for k in range(parts):

            @pl.when(turned == k)
            def _(k=k):
                outs[k][:, place] = value

        return 0

    lax.fori_loop(0, channels // LANES, one_group, 0)


def flip(value, axis, bit):
    count = lax.axis_size(axis)
    return lax.ppermute(value, axis, [(i, i ^ bit) for i in range(count)])


def entering_state(end, log_decay, tok_rows):
    place = lax.axis_index("ctx")
    count = lax.axis_size("ctx")
    prefix = jnp.zeros_like(end)
    total = end
    bit = 1
    while bit < count:
        other = flip(total, "ctx", bit)
        upper = (place & bit) != 0
        covered = (place & (bit - 1)).astype(jnp.float32) * float(tok_rows)
        prefix = prefix + jnp.where(upper, jnp.exp(-log_decay * covered) * other, 0.0)
        first = jnp.where(upper, other, total)
        second = jnp.where(upper, total, other)
        total = jnp.exp(-log_decay * float(tok_rows * bit)) * first + second
        bit *= 2
    return prefix


def in_vmem(kernel, out_shape, inputs, scratch, flops, flags=None):
    arrays = [pltpu.with_memory_space_constraint(a, pltpu.VMEM) for a in inputs]
    specs = [pl.BlockSpec(memory_space=pltpu.VMEM)] * len(arrays)
    if flags is not None:
        arrays, specs = [flags] + arrays, [pl.BlockSpec(memory_space=pltpu.SMEM)] + specs
    single = not isinstance(out_shape, tuple)
    return pl.pallas_call(
        kernel,
        out_shape=out_shape,
        in_specs=specs,
        out_specs=pl.BlockSpec(memory_space=pltpu.VMEM)
        if single
        else (pl.BlockSpec(memory_space=pltpu.VMEM),) * len(out_shape),
        scratch_shapes=scratch,
        compiler_params=pltpu.CompilerParams(vmem_limit_bytes=8 << 20),
        cost_estimate=pl.CostEstimate(flops=flops, bytes_accessed=flops // 200, transcendentals=0),
    )(*arrays)


def gated_blocks(features, short_filter, log_decay, residue, flags, parts):
    tok_rows, _, channels = features.shape
    filter_len = short_filter.shape[1]
    modes = log_decay.shape[0]
    seg_len = tok_rows // SEGS
    count = lax.axis_size("ctx")
    rim = lax.ppermute(
        features[tok_rows - (filter_len - 1) :],
        "ctx",
        [(i, i + 1) for i in range(count - 1)],
    )
    feats = jnp.transpose(features, (1, 0, 2))
    halo = jnp.transpose(rim, (1, 0, 2))
    tokens = pltpu.VMEM((seg_len, SEGS, channels), jnp.float32)
    states = pltpu.VMEM((modes, channels), jnp.float32)
    starts = pltpu.VMEM((modes, SEGS, channels), jnp.float32)
    lane_rows = pltpu.VMEM((tok_rows, LANES), jnp.float32)
    flops = 400 * tok_rows * channels * modes
    inputs = (feats, halo, short_filter, log_decay)
    driven, end, before = in_vmem(
        functools.partial(scan_kernel, seg_len),
        (tokens, states, starts),
        inputs,
        [lane_rows] * 2,
        flops,
    )
    incoming = entering_state(end, log_decay, tok_rows)
    gate, local = in_vmem(
        functools.partial(local_kernel, seg_len),
        (tokens, tokens),
        (*inputs, residue, driven, before),
        [lane_rows],
        flops,
    )
    out = pltpu.VMEM((tok_rows, channels // parts), jnp.bfloat16)
    return in_vmem(
        functools.partial(output_kernel, seg_len, parts),
        (out,) * parts,
        (log_decay, residue, gate, local, incoming),
        [lane_rows],
        flops,
        flags,
    )


def project_gathered(gated, residual, out_weight):
    columns = lax.all_to_all(out_weight, "tp", split_axis=1, concat_axis=0, tiled=True)
    weight = lax.all_gather(columns, "ctx", axis=0, tiled=True)
    rows = lax.all_gather(gated, "tp", axis=1, tiled=True)
    projected = jnp.dot(rows, weight, preferred_element_type=jnp.float32)
    return (residual.astype(jnp.float32) + projected).astype(jnp.bfloat16)


def fill_left(left, flags, piece, near_plane, far_plane):
    x, y = flags[1], flags[2]
    rows = near_plane[0].shape[0]
    for plane, sources in enumerate((near_plane, far_plane)):
        for token, source in enumerate(sources):
            for xr in range(2):
                for yr in range(2):
                    at = jnp.bitwise_xor(x, xr) * 2 + jnp.bitwise_xor(y, yr)
                    place = ((plane * 2 + xr) * 2 + yr) * piece
                    left[pl.ds(token * rows, rows), pl.ds(place, piece)] = source[
                        :, pl.ds(pl.multiple_of(at * piece, piece), piece)
                    ]


def cube_kernel(piece, chunked, part, flags, own_c, own_o, other_c, other_o, *refs):
    weights, (theirs, mine, left) = refs[:-3], refs[-3:]
    width = mine.shape[1]
    full = weights[0].shape[1] // 2
    tile = min(width, 256)
    own, other = (own_c, own_o), (other_c, other_o)

    @pl.when(flags[3] == 1)
    def _():
        fill_left(left, flags, piece, own, other)

    @pl.when(flags[3] == 0)
    def _():
        fill_left(left, flags, piece, other, own)

    for side, out in ((1 - flags[0], theirs), (flags[0], mine)):

        def one_tile(i, _, side=side, out=out):
            def columns(k):
                first = side * width if chunked[k] else side * full + part * width
                return pl.ds(pl.multiple_of(first + i * tile, tile), tile)

            right = jnp.concatenate([w[:, columns(k)] for k, w in enumerate(weights)], axis=0)
            total = jnp.dot(left[...], right, preferred_element_type=jnp.float32)
            out[:, pl.ds(pl.multiple_of(i * tile, tile), tile)] = total.astype(out.dtype)
            return 0

        lax.fori_loop(0, width // tile, one_tile, 0)


def cube_product(flags, gated, weights, piece, width, part):
    rows = 2 * gated[0].shape[0]
    depth = sum(w.shape[0] for w, _ in weights)
    return in_vmem(
        functools.partial(cube_kernel, piece, [chunked for _, chunked in weights], part),
        (pltpu.VMEM((rows, width), jnp.bfloat16), pltpu.VMEM((rows, width), jnp.float32)),
        (*gated, *[w for w, _ in weights]),
        [pltpu.VMEM((rows, depth), jnp.bfloat16)],
        4 * rows * width * depth,
        flags,
    )


def cube_place():
    c, t = lax.axis_index("ctx"), lax.axis_index("tp")
    core, y = t & 1, t >> 1
    x, zp, zh = c & 1, (c >> 1) & 1, c >> 2
    return core, y, x, zp, zh


def project_cube(mine, sib, flags, residual, out_weight, chunks):
    ctx, tp = lax.axis_size("ctx"), lax.axis_size("tp")
    core, y, _, zp, _ = cube_place()
    piece, columns = out_weight.shape
    channels = columns // tp
    width = channels // chunks

    sides = [out_weight[:, : 2 * channels], out_weight[:, 2 * channels :]]
    near = jnp.where(y == 0, sides[0], sides[1])
    give = jnp.where(y == 0, sides[1], sides[0])

    def cut_rows(value, cuts):
        return [value[lo:hi] for lo, hi in zip([0] + cuts, cuts + [piece])]

    near_z = [flip(w, "ctx", 4) for w in cut_rows(near, [piece * Z_CUT // 8])]
    near_x = [flip(w, "ctx", 1) for w in cut_rows(near, [piece * X_CUT // 8])]
    take = flip(give, "tp", 2)

    def part_of(value, j):
        starts = [k * channels + j * width for k in range(2)]
        return jnp.concatenate([value[:, at : at + width] for at in starts], axis=1)

    take_z = [flip(part_of(take, j), "ctx", 4) for j in range(chunks)]
    take_x = flip(take, "ctx", 1)
    near_zx = [flip(w, "ctx", 1) for w in near_z]
    take_zx = [flip(take_z[j], "ctx", 1) for j in range(chunks)]

    stays = core == zp
    pairs_1, pairs_2, pairs_3 = [], [], []
    for ci in range(ctx):
        for ti in range(tp):
            source = ci * tp + ti
            if (ti & 1) == ((ci >> 1) & 1):
                pairs_1.append((source, ci * tp + (ti ^ 1)))
            else:
                pairs_2.append((source, (ci ^ 2) * tp + ti))
                pairs_3.append((source, (ci ^ 2) * tp + (ti ^ 1)))

    def move(value, pairs):
        return lax.ppermute(value, ("ctx", "tp"), pairs)

    from_core = move(sib, pairs_1)
    from_z = move(mine, pairs_2)
    from_both = move(sib, pairs_3)
    own_c = jnp.where(stays, mine, from_core)
    own_o = jnp.where(stays, from_z, from_both)
    other_c = flip(own_c, "tp", 2)
    other_o = flip(own_o, "tp", 2)
    gated = (own_c, own_o, other_c, other_o)

    rows = residual.shape[0]
    outs = []
    for j in range(chunks):
        weights = [(w, False) for w in (near, take, *near_x, take_x, *near_z)]
        weights += [(take_z[j], True)] + [(w, False) for w in near_zx] + [(take_zx[j], True)]
        theirs, ours = cube_product(flags, gated, weights, piece, width, j)
        total = ours + flip(theirs, "tp", 1).astype(jnp.float32)
        pair = flip(total[rows:].astype(jnp.bfloat16), "ctx", 2)
        base = residual[:, j * width : (j + 1) * width].astype(jnp.float32)
        outs.append((base + (total[:rows] + pair.astype(jnp.float32))).astype(jnp.bfloat16))
    return jnp.concatenate(outs, axis=1)


def on_device(features, short_filter, log_decay, residue, residual, out_weight):
    ctx, tp = lax.axis_size("ctx"), lax.axis_size("tp")
    piece = out_weight.shape[0]
    if cube_shaped(ctx, tp) and piece == LANES:
        core, y, x, _, zh = cube_place()
        flags = jnp.stack([core, x, y, (y == zh).astype(jnp.int32)]).astype(jnp.int32)
        mine, sib = gated_blocks(features, short_filter, log_decay, residue, flags, 2)
        return project_cube(mine, sib, flags, residual, out_weight, CHUNKS)
    flags = jnp.zeros((1,), jnp.int32)
    (gated,) = gated_blocks(features, short_filter, log_decay, residue, flags, 1)
    return project_gathered(gated, residual, out_weight)


def cube_shaped(ctx, tp):
    return tp == 4 and ctx == 2 * tp


def solution(mesh):
    return jax.shard_map(
        on_device,
        mesh=mesh,
        in_specs=(
            P("ctx", None, "tp"),
            P(None, None, "tp"),
            P(None, "tp"),
            P(None, "tp"),
            P("ctx", "tp"),
            P(("ctx", "tp"), None),
        ),
        out_specs=P("ctx", "tp"),
        check_vma=False,
    )
```

profile of v0, /device:TPU:0, one launch (start us, length us, event | category | flops | bytes accessed | tf_op | source)
XLA Modules:
  0.0 122.0 jit_solution(16836754194388045276)
XLA Ops:
  0.8 4.9 %collective-permute-start = (bf16[2,3,1024]{2,0,1:T(2,128)(2,1)S(1)}, bf16[2,3,1024]{2,0,1:T(2,128)(2,1)S(1)}, u32[]{:S(2)}, u32[]{:S(2)}) collective-permute-start(bf16[2,3,1024]{2,0,1:T(2,128)(2,1)S(1)} %slice.54), channel_id=1, source_target_pairs={{0,4},{4,8},{8,12},{12,16},{16,20},{20,24},{24,28},{1,5},{5,9},{9,... | collective-permute-start | bytes 36872 | tf_op jit(solution)/shard_map/ppermute | solution.py:231
  10.1 3.1 %shard_map.64 = (f32[32,8,1024]{2,1,0:T(8,128)S(1)}, f32[16,1024]{1,0:T(8,128)S(1)}, f32[16,8,1024]{2,1,0:T(8,128)S(1)}) custom-call(bf16[3,256,1024]{2,1,0:T(8,128)(2,1)S(1)} %bitcast.6, bf16[3,2,1024]{2,1,0:T(2,128)(2,1)S(1)} %bitcast.8, f32[3,3,1024]{2,1,0:T(4,128)S(1)} %copy-done.5, f32[16,1024]{1,0:T(8,128)S(1)} %copy-done), custom_call_target="tpu_custom_call" | custom-call | flops 1677721600 | bytes 8388608 | tf_op jit(solution)/shard_map/pallas_call | solution.py:212
  15.0 2.4 %collective-permute-start.1 = (f32[16,1024]{1,0:T(8,128)S(1)}, f32[16,1024]{1,0:T(8,128)S(1)}, u32[]{:S(2)}, u32[]{:S(2)}) collective-permute-start(f32[16,1024]{1,0:T(8,128)S(1)} %get-tuple-element.20), channel_id=1, source_target_pairs={{0,4},{4,0},{8,12},{12,8},{16,20},{20,16},{24,28},{28,24},{1,5},{5... | collective-permute-start | bytes 196616 | tf_op jit(solution)/shard_map/ppermute | solution.py:185
  18.3 1.5 %collective-permute-start.9 = (bf16[128,2048]{1,0:T(8,128)(2,1)}, bf16[128,2048]{1,0:T(8,128)(2,1)S(1)}, u32[]{:S(2)}, u32[]{:S(2)}) collective-permute-start(bf16[128,2048]{1,0:T(8,128)(2,1)} %get-tuple-element.27), channel_id=1, source_target_pairs={{0,2},{1,3},{2,0},{3,1},{4,6},{5,7},{6,4},{7,5},{8,10},{9,11},{10,... | collective-permute-start | bytes 1572872 | tf_op jit(solution)/shard_map/ppermute | solution.py:185
  20.6 2.6 %collective-permute-start.13 = (bf16[96,2048]{1,0:T(8,128)(2,1)}, bf16[96,2048]{1,0:T(8,128)(2,1)S(1)}, u32[]{:S(2)}, u32[]{:S(2)}) collective-permute-start(bf16[96,2048]{1,0:T(8,128)(2,1)} %slice.72), channel_id=1, source_target_pairs={{0,16},{4,20},{8,24},{12,28},{16,0},{20,4},{24,8},{28,12},{1,17},{... | collective-permute-start | bytes 1179656 | tf_op jit(solution)/shard_map/ppermute | solution.py:185
  24.2 1.6 %collective-permute-start.2 = (f32[16,1024]{1,0:T(8,128)S(1)}, f32[16,1024]{1,0:T(8,128)S(1)}, u32[]{:S(2)}, u32[]{:S(2)}) collective-permute-start(f32[16,1024]{1,0:T(8,128)S(1)} %select_add_fusion.2), channel_id=1, source_target_pairs={{0,8},{4,12},{8,0},{12,4},{16,24},{20,28},{24,16},{28,20},{1,9},{5... | collective-permute-start | bytes 196616 | tf_op jit(solution)/shard_map/ppermute | solution.py:185
  25.9 8.5 %collective-permute-done.2 = f32[16,1024]{1,0:T(8,128)S(1)} collective-permute-done((f32[16,1024]{1,0:T(8,128)S(1)}, f32[16,1024]{1,0:T(8,128)S(1)}, u32[]{:S(2)}, u32[]{:S(2)}) %collective-permute-start.2) | collective-permute-done | bytes 65568 | tf_op jit(solution)/shard_map/ppermute | solution.py:185
  34.4 2.3 %collective-permute-start.3 = (f32[16,1024]{1,0:T(8,128)S(1)}, f32[16,1024]{1,0:T(8,128)S(1)}, u32[]{:S(2)}, u32[]{:S(2)}) collective-permute-start(f32[16,1024]{1,0:T(8,128)S(1)} %select_add_fusion.1), channel_id=1, source_target_pairs={{0,16},{4,20},{8,24},{12,28},{16,0},{20,4},{24,8},{28,12},{1,17},{... | collective-permute-start | bytes 196616 | tf_op jit(solution)/shard_map/ppermute | solution.py:185
  39.0 3.3 %shard_map.65 = (f32[32,8,1024]{2,1,0:T(8,128)S(1)}, f32[32,8,1024]{2,1,0:T(8,128)S(1)}) custom-call(bf16[3,256,1024]{2,1,0:T(8,128)(2,1)S(1)} %bitcast.7, bf16[3,2,1024]{2,1,0:T(2,128)(2,1)S(1)} %bitcast.9, f32[3,3,1024]{2,1,0:T(4,128)S(1)} %copy-done.6, f32[16,1024]{1,0:T(8,128)S(1)} %copy-done.1, f32[16,1024]{1,0:T(8,128)S(1)} %copy-done.4, ...), custom_call_target="tpu_custom_call" | custom-call | flops 1677721600 | bytes 8388608 | tf_op jit(solution)/shard_map/pallas_call | solution.py:212
  42.3 5.3 %collective-permute-done.3 = f32[16,1024]{1,0:T(8,128)S(1)} collective-permute-done((f32[16,1024]{1,0:T(8,128)S(1)}, f32[16,1024]{1,0:T(8,128)S(1)}, u32[]{:S(2)}, u32[]{:S(2)}) %collective-permute-start.3) | collective-permute-done | bytes 65568 | tf_op jit(solution)/shard_map/ppermute | solution.py:185
  47.7 2.3 %shard_map.66 = (bf16[256,512]{1,0:T(8,128)(2,1)S(1)}, bf16[256,512]{1,0:T(8,128)(2,1)S(1)}) custom-call(s32[4]{0:T(128)S(1)} %pad_add_fusion.flags, f32[16,1024]{1,0:T(8,128)S(1)} %copy-done.1, f32[16,1024]{1,0:T(8,128)S(1)} %copy-done.4, f32[32,8,1024]{2,1,0:T(8,128)S(1)} %get-tuple-element.18.gate, f32[32,8,1024]{2,1,0:T(8,128)S(1)} %get-tuple-element.19.local, ...), custom_call_target="tpu_custom_call" | custom-call | flops 1677721600 | bytes 8388608 | tf_op jit(solution)/shard_map/pallas_call | solution.py:212
  53.5 4.8 %collective-permute-done.5 = bf16[256,512]{1,0:T(8,128)(2,1)S(1)} collective-permute-done((bf16[256,512]{1,0:T(8,128)(2,1)S(1)}, bf16[256,512]{1,0:T(8,128)(2,1)S(1)}, u32[]{:S(2)}, u32[]{:S(2)}) %collective-permute-start.5) | collective-permute-done | bytes 262176 | tf_op jit(solution)/shard_map/ppermute | solution.py:381
  60.3 3.6 %collective-permute-start.4 = (bf16[256,512]{1,0:T(8,128)(2,1)S(1)}, bf16[256,512]{1,0:T(8,128)(2,1)S(1)}, u32[]{:S(2)}, u32[]{:S(2)}) collective-permute-start(bf16[256,512]{1,0:T(8,128)(2,1)S(1)} %get-tuple-element.22), channel_id=1, source_target_pairs={{0,1},{2,3},{4,5},{6,7},{9,8},{11,10},{13,12},{15,14},{16,17},{18,... | collective-permute-start | bytes 786440 | tf_op jit(solution)/shard_map/ppermute | solution.py:381
  64.7 5.5 %collective-permute-done.17.refs_9_ = bf16[32,2048]{1,0:T(8,128)(2,1)S(1)} collective-permute-done((bf16[32,2048]{1,0:T(8,128)(2,1)S(1)}, bf16[32,2048]{1,0:T(8,128)(2,1)S(1)}, u32[]{:S(2)}, u32[]{:S(2)}) %collective-permute-start.17) | collective-permute-done | bytes 131104 | tf_op jit(solution)/shard_map/ppermute | solution.py:185
  73.7 1.5 %collective-permute-start.15 = (bf16[128,1024]{1,0:T(8,128)(2,1)S(1)}, bf16[128,1024]{1,0:T(8,128)(2,1)S(1)}, u32[]{:S(2)}, u32[]{:S(2)}) collective-permute-start(bf16[128,1024]{1,0:T(8,128)(2,1)S(1)} %pad_maximum_fusion.1), channel_id=1, source_target_pairs={{0,16},{4,20},{8,24},{12,28},{16,0},{20,4},{24,8},{28,12},{1,17},{... | collective-permute-start | bytes 786440 | tf_op jit(solution)/shard_map/ppermute | solution.py:185
  75.2 2.7 %collective-permute-done.8.other_o = bf16[256,512]{1,0:T(8,128)(2,1)S(1)} collective-permute-done((bf16[256,512]{1,0:T(8,128)(2,1)S(1)}, bf16[256,512]{1,0:T(8,128)(2,1)S(1)}, u32[]{:S(2)}, u32[]{:S(2)}) %collective-permute-start.8) | collective-permute-done | bytes 262176 | tf_op jit(solution)/shard_map/ppermute | solution.py:185
  78.5 11.3 %collective-permute-done.21.refs_7_ = bf16[128,1024]{1,0:T(8,128)(2,1)S(1)} collective-permute-done((bf16[128,1024]{1,0:T(8,128)(2,1)S(1)}, bf16[128,1024]{1,0:T(8,128)(2,1)S(1)}, u32[]{:S(2)}, u32[]{:S(2)}) %collective-permute-start.21) | collective-permute-done | bytes 262176 | tf_op jit(solution)/shard_map/ppermute | solution.py:185
  91.2 4.1 %collective-permute-done.15.refs_7_ = bf16[128,1024]{1,0:T(8,128)(2,1)S(1)} collective-permute-done((bf16[128,1024]{1,0:T(8,128)(2,1)S(1)}, bf16[128,1024]{1,0:T(8,128)(2,1)S(1)}, u32[]{:S(2)}, u32[]{:S(2)}) %collective-permute-start.15) | collective-permute-done | bytes 262176 | tf_op jit(solution)/shard_map/ppermute | solution.py:185
  97.9 2.6 %shard_map.68 = (bf16[512,512]{1,0:T(8,128)(2,1)S(1)}, f32[512,512]{1,0:T(8,128)S(1)}) custom-call(s32[4]{0:T(128)S(1)} %pad_add_fusion.flags, bf16[256,512]{1,0:T(8,128)(2,1)S(1)} %broadcast_select_fusion.3.own_c, bf16[256,512]{1,0:T(8,128)(2,1)S(1)} %broadcast_select_fusion.2.own_o, bf16[256,512]{1,0:T(8,128)(2,1)S(1)} %collective-permute-done.7.other_c, ...), custom_call_target="tpu_custom_call" | custom-call | flops 1073741824 | bytes 5368709 | tf_op jit(solution)/shard_map/pallas_call | solution.py:212
  100.6 2.9 %collective-permute-done.18.refs_10_ = bf16[128,1024]{1,0:T(8,128)(2,1)S(1)} collective-permute-done((bf16[128,1024]{1,0:T(8,128)(2,1)S(1)}, bf16[128,1024]{1,0:T(8,128)(2,1)S(1)}, u32[]{:S(2)}, u32[]{:S(2)}) %collective-permute-start.18) | collective-permute-done | bytes 262176 | tf_op jit(solution)/shard_map/ppermute | solution.py:185
  103.5 2.6 %shard_map.67 = (bf16[512,512]{1,0:T(8,128)(2,1)S(1)}, f32[512,512]{1,0:T(8,128)S(1)}) custom-call(s32[4]{0:T(128)S(1)} %pad_add_fusion.flags, bf16[256,512]{1,0:T(8,128)(2,1)S(1)} %broadcast_select_fusion.3.own_c, bf16[256,512]{1,0:T(8,128)(2,1)S(1)} %broadcast_select_fusion.2.own_o, bf16[256,512]{1,0:T(8,128)(2,1)S(1)} %collective-permute-done.7.other_c, ...), custom_call_target="tpu_custom_call" | custom-call | flops 1073741824 | bytes 5368709 | tf_op jit(solution)/shard_map/pallas_call | solution.py:212
  106.5 1.6 %collective-permute-done.19 = bf16[512,512]{1,0:T(8,128)(2,1)S(1)} collective-permute-done((bf16[512,512]{1,0:T(8,128)(2,1)S(1)}, bf16[512,512]{1,0:T(8,128)(2,1)S(1)}, u32[]{:S(2)}, u32[]{:S(2)}) %collective-permute-start.19) | collective-permute-done | bytes 524320 | tf_op jit(solution)/shard_map/ppermute | solution.py:185
  108.8 6.9 %collective-permute-done.24 = bf16[256,512]{1,0:T(8,128)(2,1)S(1)} collective-permute-done((bf16[256,512]{1,0:T(8,128)(2,1)S(1)}, bf16[256,512]{1,0:T(8,128)(2,1)S(1)}, u32[]{:S(2)}, u32[]{:S(2)}) %collective-permute-start.24) | collective-permute-done | bytes 262176 | tf_op jit(solution)/shard_map/ppermute | solution.py:185
  115.7 5.1 %collective-permute-done.20 = bf16[256,512]{1,0:T(8,128)(2,1)S(1)} collective-permute-done((bf16[256,512]{1,0:T(8,128)(2,1)S(1)}, bf16[256,512]{1,0:T(8,128)(2,1)S(1)}, u32[]{:S(2)}, u32[]{:S(2)}) %collective-permute-start.20) | collective-permute-done | bytes 262176 | tf_op jit(solution)/shard_map/ppermute | solution.py:185
  (77 shorter events, 28.6 us)
Async XLA Ops:
  0.8 6.3 %collective-permute-start = (bf16[2,3,1024]{2,0,1:T(2,128)(2,1)S(1)}, bf16[2,3,1024]{2,0,1:T(2,128)(2,1)S(1)}, u32[]{:S(2)}, u32[]{:S(2)}) collective-permute-start(bf16[2,3,1024]{2,0,1:T(2,128)(2,1)S(1)} %slice.54), channel_id=1, source_target_pairs={{0,4},{4,8},{8,12},{12,16},{16,20},{20,24},{24,28},{1,5},{5,9},{9,... | collective-permute-start | bytes 36872 | tf_op jit(solution)/shard_map/ppermute | solution.py:231
  15.0 9.1 %collective-permute-start.1 = (f32[16,1024]{1,0:T(8,128)S(1)}, f32[16,1024]{1,0:T(8,128)S(1)}, u32[]{:S(2)}, u32[]{:S(2)}) collective-permute-start(f32[16,1024]{1,0:T(8,128)S(1)} %get-tuple-element.20), channel_id=1, source_target_pairs={{0,4},{4,0},{8,12},{12,8},{16,20},{20,16},{24,28},{28,24},{1,5},{5... | collective-permute-start | bytes 196616 | tf_op jit(solution)/shard_map/ppermute | solution.py:185
  18.3 45.7 %collective-permute-start.9 = (bf16[128,2048]{1,0:T(8,128)(2,1)}, bf16[128,2048]{1,0:T(8,128)(2,1)S(1)}, u32[]{:S(2)}, u32[]{:S(2)}) collective-permute-start(bf16[128,2048]{1,0:T(8,128)(2,1)} %get-tuple-element.27), channel_id=1, source_target_pairs={{0,2},{1,3},{2,0},{3,1},{4,6},{5,7},{6,4},{7,5},{8,10},{9,11},{10,... | collective-permute-start | bytes 1572872 | tf_op jit(solution)/shard_map/ppermute | solution.py:185
  20.6 39.8 %collective-permute-start.13 = (bf16[96,2048]{1,0:T(8,128)(2,1)}, bf16[96,2048]{1,0:T(8,128)(2,1)S(1)}, u32[]{:S(2)}, u32[]{:S(2)}) collective-permute-start(bf16[96,2048]{1,0:T(8,128)(2,1)} %slice.72), channel_id=1, source_target_pairs={{0,16},{4,20},{8,24},{12,28},{16,0},{20,4},{24,8},{28,12},{1,17},{... | collective-permute-start | bytes 1179656 | tf_op jit(solution)/shard_map/ppermute | solution.py:185
  23.8 28.2 %collective-permute-start.14 = (bf16[32,2048]{1,0:T(8,128)(2,1)}, bf16[32,2048]{1,0:T(8,128)(2,1)S(1)}, u32[]{:S(2)}, u32[]{:S(2)}) collective-permute-start(bf16[32,2048]{1,0:T(8,128)(2,1)} %slice.73), channel_id=1, source_target_pairs={{0,16},{4,20},{8,24},{12,28},{16,0},{20,4},{24,8},{28,12},{1,17},{... | collective-permute-start | bytes 393224 | tf_op jit(solution)/shard_map/ppermute | solution.py:185
  24.2 10.2 %collective-permute-start.2 = (f32[16,1024]{1,0:T(8,128)S(1)}, f32[16,1024]{1,0:T(8,128)S(1)}, u32[]{:S(2)}, u32[]{:S(2)}) collective-permute-start(f32[16,1024]{1,0:T(8,128)S(1)} %select_add_fusion.2), channel_id=1, source_target_pairs={{0,8},{4,12},{8,0},{12,4},{16,24},{20,28},{24,16},{28,20},{1,9},{5... | collective-permute-start | bytes 196616 | tf_op jit(solution)/shard_map/ppermute | solution.py:185
  34.4 13.3 %collective-permute-start.3 = (f32[16,1024]{1,0:T(8,128)S(1)}, f32[16,1024]{1,0:T(8,128)S(1)}, u32[]{:S(2)}, u32[]{:S(2)}) collective-permute-start(f32[16,1024]{1,0:T(8,128)S(1)} %select_add_fusion.1), channel_id=1, source_target_pairs={{0,16},{4,20},{8,24},{12,28},{16,0},{20,4},{24,8},{28,12},{1,17},{... | collective-permute-start | bytes 196616 | tf_op jit(solution)/shard_map/ppermute | solution.py:185
  50.0 8.3 %collective-permute-start.5 = (bf16[256,512]{1,0:T(8,128)(2,1)S(1)}, bf16[256,512]{1,0:T(8,128)(2,1)S(1)}, u32[]{:S(2)}, u32[]{:S(2)}) collective-permute-start(bf16[256,512]{1,0:T(8,128)(2,1)S(1)} %get-tuple-element.21), channel_id=1, source_target_pairs={{1,9},{3,11},{5,13},{7,15},{8,0},{10,2},{12,4},{14,6},{17,25},{19,... | collective-permute-start | bytes 786440 | tf_op jit(solution)/shard_map/ppermute | solution.py:381
  51.3 8.3 %collective-permute-start.6 = (bf16[256,512]{1,0:T(8,128)(2,1)S(1)}, bf16[256,512]{1,0:T(8,128)(2,1)S(1)}, u32[]{:S(2)}, u32[]{:S(2)}) collective-permute-start(bf16[256,512]{1,0:T(8,128)(2,1)S(1)} %get-tuple-element.22), channel_id=1, source_target_pairs={{1,8},{3,10},{5,12},{7,14},{8,1},{10,3},{12,5},{14,7},{17,24},{19,... | collective-permute-start | bytes 786440 | tf_op jit(solution)/shard_map/ppermute | solution.py:381
  52.0 18.7 %collective-permute-start.10 = (bf16[64,2048]{1,0:T(8,128)(2,1)S(1)}, bf16[64,2048]{1,0:T(8,128)(2,1)S(1)}, u32[]{:S(2)}, u32[]{:S(2)}) collective-permute-start(bf16[64,2048]{1,0:T(8,128)(2,1)S(1)} %get-tuple-element.36), channel_id=1, source_target_pairs={{0,4},{4,0},{8,12},{12,8},{16,20},{20,16},{24,28},{28,24},{1,5},{5... | collective-permute-start | bytes 786440 | tf_op jit(solution)/shard_map/ppermute | solution.py:185
  58.3 15.4 %collective-permute-start.11 = (bf16[64,2048]{1,0:T(8,128)(2,1)S(1)}, bf16[64,2048]{1,0:T(8,128)(2,1)S(1)}, u32[]{:S(2)}, u32[]{:S(2)}) collective-permute-start(bf16[64,2048]{1,0:T(8,128)(2,1)S(1)} %get-tuple-element.35), channel_id=1, source_target_pairs={{0,4},{4,0},{8,12},{12,8},{16,20},{20,16},{24,28},{28,24},{1,5},{5... | collective-permute-start | bytes 786440 | tf_op jit(solution)/shard_map/ppermute | solution.py:185
  59.6 10.6 %collective-permute-start.17 = (bf16[32,2048]{1,0:T(8,128)(2,1)S(1)}, bf16[32,2048]{1,0:T(8,128)(2,1)S(1)}, u32[]{:S(2)}, u32[]{:S(2)}) collective-permute-start(bf16[32,2048]{1,0:T(8,128)(2,1)S(1)} %collective-permute-done.14.refs_6_), channel_id=1, source_target_pairs={{0,4},{4,0},{8,12},{12,8},{16,20},{20,16},{24,28},{28,24},{1,5},{5... | collective-permute-start | bytes 393224 | tf_op jit(solution)/shard_map/ppermute | solution.py:185
  60.3 11.8 %collective-permute-start.4 = (bf16[256,512]{1,0:T(8,128)(2,1)S(1)}, bf16[256,512]{1,0:T(8,128)(2,1)S(1)}, u32[]{:S(2)}, u32[]{:S(2)}) collective-permute-start(bf16[256,512]{1,0:T(8,128)(2,1)S(1)} %get-tuple-element.22), channel_id=1, source_target_pairs={{0,1},{2,3},{4,5},{6,7},{9,8},{11,10},{13,12},{15,14},{16,17},{18,... | collective-permute-start | bytes 786440 | tf_op jit(solution)/shard_map/ppermute | solution.py:381
  64.0 32.8 %collective-permute-start.16 = (bf16[96,2048]{1,0:T(8,128)(2,1)S(1)}, bf16[96,2048]{1,0:T(8,128)(2,1)S(1)}, u32[]{:S(2)}, u32[]{:S(2)}) collective-permute-start(bf16[96,2048]{1,0:T(8,128)(2,1)S(1)} %collective-permute-done.13.refs_5_), channel_id=1, source_target_pairs={{0,4},{4,0},{8,12},{12,8},{16,20},{20,16},{24,28},{28,24},{1,5},{5... | collective-permute-start | bytes 1179656 | tf_op jit(solution)/shard_map/ppermute | solution.py:185
  70.2 7.7 %collective-permute-start.8 = (bf16[256,512]{1,0:T(8,128)(2,1)S(1)}, bf16[256,512]{1,0:T(8,128)(2,1)S(1)}, u32[]{:S(2)}, u32[]{:S(2)}) collective-permute-start(bf16[256,512]{1,0:T(8,128)(2,1)S(1)} %broadcast_select_fusion.2.own_o), channel_id=1, source_target_pairs={{0,2},{1,3},{2,0},{3,1},{4,6},{5,7},{6,4},{7,5},{8,10},{9,11},{10,... | collective-permute-start | bytes 786440 | tf_op jit(solution)/shard_map/ppermute | solution.py:185
  70.8 19.0 %collective-permute-start.21 = (bf16[128,1024]{1,0:T(8,128)(2,1)S(1)}, bf16[128,1024]{1,0:T(8,128)(2,1)S(1)}, u32[]{:S(2)}, u32[]{:S(2)}) collective-permute-start(bf16[128,1024]{1,0:T(8,128)(2,1)S(1)} %pad_maximum_fusion.2), channel_id=1, source_target_pairs={{0,16},{4,20},{8,24},{12,28},{16,0},{20,4},{24,8},{28,12},{1,17},{... | collective-permute-start | bytes 786440 | tf_op jit(solution)/shard_map/ppermute | solution.py:185
  72.2 25.7 %collective-permute-start.12 = (bf16[128,2048]{1,0:T(8,128)(2,1)S(1)}, bf16[128,2048]{1,0:T(8,128)(2,1)S(1)}, u32[]{:S(2)}, u32[]{:S(2)}) collective-permute-start(bf16[128,2048]{1,0:T(8,128)(2,1)S(1)} %collective-permute-done.9.refs_1_), channel_id=1, source_target_pairs={{0,4},{4,0},{8,12},{12,8},{16,20},{20,16},{24,28},{28,24},{1,5},{5... | collective-permute-start | bytes 1572872 | tf_op jit(solution)/shard_map/ppermute | solution.py:185
  73.7 21.6 %collective-permute-start.15 = (bf16[128,1024]{1,0:T(8,128)(2,1)S(1)}, bf16[128,1024]{1,0:T(8,128)(2,1)S(1)}, u32[]{:S(2)}, u32[]{:S(2)}) collective-permute-start(bf16[128,1024]{1,0:T(8,128)(2,1)S(1)} %pad_maximum_fusion.1), channel_id=1, source_target_pairs={{0,16},{4,20},{8,24},{12,28},{16,0},{20,4},{24,8},{28,12},{1,17},{... | collective-permute-start | bytes 786440 | tf_op jit(solution)/shard_map/ppermute | solution.py:185
  78.0 18.8 %collective-permute-start.7 = (bf16[256,512]{1,0:T(8,128)(2,1)S(1)}, bf16[256,512]{1,0:T(8,128)(2,1)S(1)}, u32[]{:S(2)}, u32[]{:S(2)}) collective-permute-start(bf16[256,512]{1,0:T(8,128)(2,1)S(1)} %broadcast_select_fusion.3.own_c), channel_id=1, source_target_pairs={{0,2},{1,3},{2,0},{3,1},{4,6},{5,7},{6,4},{7,5},{8,10},{9,11},{10,... | collective-permute-start | bytes 786440 | tf_op jit(solution)/shard_map/ppermute | solution.py:185
  89.8 8.1 %collective-permute-start.22 = (bf16[128,1024]{1,0:T(8,128)(2,1)S(1)}, bf16[128,1024]{1,0:T(8,128)(2,1)S(1)}, u32[]{:S(2)}, u32[]{:S(2)}) collective-permute-start(bf16[128,1024]{1,0:T(8,128)(2,1)S(1)} %collective-permute-done.21.refs_7_), channel_id=1, source_target_pairs={{0,4},{4,0},{8,12},{12,8},{16,20},{20,16},{24,28},{28,24},{1,5},{5... | collective-permute-start | bytes 786440 | tf_op jit(solution)/shard_map/ppermute | solution.py:185
  95.3 8.2 %collective-permute-start.18 = (bf16[128,1024]{1,0:T(8,128)(2,1)S(1)}, bf16[128,1024]{1,0:T(8,128)(2,1)S(1)}, u32[]{:S(2)}, u32[]{:S(2)}) collective-permute-start(bf16[128,1024]{1,0:T(8,128)(2,1)S(1)} %collective-permute-done.15.refs_7_), channel_id=1, source_target_pairs={{0,4},{4,0},{8,12},{12,8},{16,20},{20,16},{24,28},{28,24},{1,5},{5... | collective-permute-start | bytes 786440 | tf_op jit(solution)/shard_map/ppermute | solution.py:185
  100.6 5.7 %collective-permute-start.23 = (bf16[512,512]{1,0:T(8,128)(2,1)S(1)}, bf16[512,512]{1,0:T(8,128)(2,1)S(1)}, u32[]{:S(2)}, u32[]{:S(2)}) collective-permute-start(bf16[512,512]{1,0:T(8,128)(2,1)S(1)} %get-tuple-element.26), channel_id=1, source_target_pairs={{0,1},{1,0},{2,3},{3,2},{4,5},{5,4},{6,7},{7,6},{8,9},{9,8},{10,11... | collective-permute-start | bytes 1572872 | tf_op jit(solution)/shard_map/ppermute | solution.py:185
  106.5 9.2 %collective-permute-start.24 = (bf16[256,512]{1,0:T(8,128)(2,1)S(1)}, bf16[256,512]{1,0:T(8,128)(2,1)S(1)}, u32[]{:S(2)}, u32[]{:S(2)}) collective-permute-start(bf16[256,512]{1,0:T(8,128)(2,1)S(1)} %slice.100), channel_id=1, source_target_pairs={{0,8},{4,12},{8,0},{12,4},{16,24},{20,28},{24,16},{28,20},{1,9},{5... | collective-permute-start | bytes 786440 | tf_op jit(solution)/shard_map/ppermute | solution.py:185
  108.4 12.5 %collective-permute-start.20 = (bf16[256,512]{1,0:T(8,128)(2,1)S(1)}, bf16[256,512]{1,0:T(8,128)(2,1)S(1)}, u32[]{:S(2)}, u32[]{:S(2)}) collective-permute-start(bf16[256,512]{1,0:T(8,128)(2,1)S(1)} %slice.101), channel_id=1, source_target_pairs={{0,8},{4,12},{8,0},{12,4},{16,24},{20,28},{24,16},{28,20},{1,9},{5... | collective-permute-start | bytes 786440 | tf_op jit(solution)/shard_map/ppermute | solution.py:185
  (14 other events, 103.4 us)
where the time goes:
time: 122 us
  waiting for transfers between devices  61.3 us (50%)
  starting transfers between devices  34.4 us (28%)
  Pallas kernels  13.9 us (11%)
  local copies, waits for them, and re-layouts  9.53 us (8%)
  other arithmetic  2.59 us (2%)
    ppermute x21, waiting for transfers between devices, flip(): return lax.ppermute(value, axis, [(i, i ^ bit) for i in range(count)])  55.2 us
    ppermute x21, starting transfers between devices, flip(): return lax.ppermute(value, axis, [(i, i ^ bit) for i in range(count)])  23.9 us
    pallas_call x5, Pallas kernels, in_vmem(): pl.pallas_call(kernel, out_shape=out_shape, in_specs=specs, out_specs=pl....  13.9 us
    unnamed x26, local copies, waits for them, and re-layouts  7.13 us
    ppermute x3, starting transfers between devices, move(): return lax.ppermute(value, ('ctx', 'tp'), pairs)  5.59 us
    ppermute x1, starting transfers between devices, gated_blocks(): lax.ppermute(features[tok_rows - (filter_len - 1):], 'ctx', [(i, i + 1) f...  4.87 us
    ppermute x3, waiting for transfers between devices, move(): return lax.ppermute(value, ('ctx', 'tp'), pairs)  4.77 us
  transfers between devices with their start and end apart: 25, of which 13 were waited for; matrix products, arithmetic and copies ran while one was open for 3% of the time, Pallas kernels for 9%

commit v1 on v0

--- a/solution.py
+++ b/solution.py
@@ -11,7 +11,8 @@
 LANES = 128
 CHUNKS = 2
 UNROLL = 16
-Z_CUT, X_CUT = 6, 4
+CUTS = (3,)
+CORE_FIRST, PART_FIRST, ONE_PART = range(3)
 SEGS = 8
 
 
@@ -46,7 +47,7 @@
 
 
 def scan_kernel(
-    seg_len, feats, halo, taps, decay, driven, end, before, k_rows, v_rows
+    seg_len, feats, halo, taps, decay, end, before, k_rows, v_rows
 ):
     modes, channels = decay.shape
     filter_len = taps.shape[1]
@@ -68,7 +69,6 @@
             k, k_past = filter_step(k_rows[at, :], k_past, k_taps)
             v, v_past = filter_step(v_rows[at, :], v_past, v_taps)
             drive = k * v
-            driven[i, :, lanes] = drive
             states = [a * s + drive for a, s in zip(step, states)]
             return states, k_past, v_past
 
@@ -101,7 +101,7 @@
 
 
 def local_kernel(
-    seg_len, feats, halo, taps, decay, residue, driven, before, gate, local, q_rows
+    seg_len, feats, halo, taps, decay, residue, before, gate, local, q_rows, k_rows, v_rows
 ):
     modes, channels = decay.shape
     filter_len = taps.shape[1]
@@ -113,17 +113,23 @@
         q_rows[...] = feats[0, :, lanes].astype(jnp.float32)
         step = [row(per_token, n) for n in range(modes)]
         gain = [row(weights, n) for n in range(modes)]
+        k_rows[...] = feats[1, :, lanes].astype(jnp.float32)
+        v_rows[...] = feats[2, :, lanes].astype(jnp.float32)
         q_taps = taps_of(taps, 0, lanes, filter_len)
+        k_taps = taps_of(taps, 1, lanes, filter_len)
+        v_taps = taps_of(taps, 2, lanes, filter_len)
 
         def one_token(i, carry):
-            states, q_past = carry
+            states, q_past, k_past, v_past = carry
             at = pl.ds(i, SEGS, stride=seg_len)
             now, q_past = filter_step(q_rows[at, :], q_past, q_taps)
+            k, k_past = filter_step(k_rows[at, :], k_past, k_taps)
+            v, v_past = filter_step(v_rows[at, :], v_past, v_taps)
             gate[i, :, lanes] = now
-            drive = driven[i, :, lanes]
+            drive = k * v
             states = [a * s + drive for a, s in zip(step, states)]
             local[i, :, lanes] = tree_sum([r * s for r, s in zip(gain, states)])
-            return states, q_past
+            return states, q_past, k_past, v_past
 
         lax.fori_loop(
             0,
@@ -132,6 +138,8 @@
             (
                 [before[n, :, lanes] for n in range(modes)],
                 history(q_rows, halo, 0, lanes, seg_len, filter_len),
+                history(k_rows, halo, 1, lanes, seg_len, filter_len),
+                history(v_rows, halo, 2, lanes, seg_len, filter_len),
             ),
             unroll=UNROLL,
         )
@@ -241,19 +249,15 @@
     lane_rows = pltpu.VMEM((tok_rows, LANES), jnp.float32)
     flops = 400 * tok_rows * channels * modes
     inputs = (feats, halo, short_filter, log_decay)
-    driven, end, before = in_vmem(
-        functools.partial(scan_kernel, seg_len),
-        (tokens, states, starts),
-        inputs,
-        [lane_rows] * 2,
-        flops,
+    end, before = in_vmem(
+        functools.partial(scan_kernel, seg_len), (states, starts), inputs, [lane_rows] * 2, flops
     )
     incoming = entering_state(end, log_decay, tok_rows)
     gate, local = in_vmem(
         functools.partial(local_kernel, seg_len),
         (tokens, tokens),
-        (*inputs, residue, driven, before),
-        [lane_rows],
+        (*inputs, residue, before),
+        [lane_rows] * 3,
         flops,
     )
     out = pltpu.VMEM((tok_rows, channels // parts), jnp.bfloat16)
@@ -289,7 +293,7 @@
                     ]
 
 
-def cube_kernel(piece, chunked, part, flags, own_c, own_o, other_c, other_o, *refs):
+def cube_kernel(piece, orders, part, flags, own_c, own_o, other_c, other_o, *refs):
     weights, (theirs, mine, left) = refs[:-3], refs[-3:]
     width = mine.shape[1]
     full = weights[0].shape[1] // 2
@@ -308,7 +312,11 @@
 
         def one_tile(i, _, side=side, out=out):
             def columns(k):
-                first = side * width if chunked[k] else side * full + part * width
+                first = {
+                    CORE_FIRST: side * full + part * width,
+                    PART_FIRST: (2 * part + side) * width,
+                    ONE_PART: side * width,
+                }[orders[k]]
                 return pl.ds(pl.multiple_of(first + i * tile, tile), tile)
 
             right = jnp.concatenate([w[:, columns(k)] for k, w in enumerate(weights)], axis=0)
@@ -323,7 +331,7 @@
     rows = 2 * gated[0].shape[0]
     depth = sum(w.shape[0] for w, _ in weights)
     return in_vmem(
-        functools.partial(cube_kernel, piece, [chunked for _, chunked in weights], part),
+        functools.partial(cube_kernel, piece, [order for _, order in weights], part),
         (pltpu.VMEM((rows, width), jnp.bfloat16), pltpu.VMEM((rows, width), jnp.float32)),
         (*gated, *[w for w, _ in weights]),
         [pltpu.VMEM((rows, depth), jnp.bfloat16)],
@@ -347,21 +355,20 @@
     width = channels // chunks
 
     sides = [out_weight[:, : 2 * channels], out_weight[:, 2 * channels :]]
-    near = jnp.where(y == 0, sides[0], sides[1])
-    give = jnp.where(y == 0, sides[1], sides[0])
-
-    def cut_rows(value, cuts):
-        return [value[lo:hi] for lo, hi in zip([0] + cuts, cuts + [piece])]
-
-    near_z = [flip(w, "ctx", 4) for w in cut_rows(near, [piece * Z_CUT // 8])]
-    near_x = [flip(w, "ctx", 1) for w in cut_rows(near, [piece * X_CUT // 8])]
+    cuts = [0] + [piece * k // 8 for k in CUTS] + [piece]
+    near = [
+        jnp.where(y == 0, sides[0][lo:hi], sides[1][lo:hi]) for lo, hi in zip(cuts, cuts[1:])
+    ]
+
+    def parts_first(side):
+        starts = [k * channels + j * width for j in range(chunks) for k in range(2)]
+        return jnp.concatenate([side[:, at : at + width] for at in starts], axis=1)
+
+    give = jnp.where(y == 0, parts_first(sides[1]), parts_first(sides[0]))
+    near_z = [flip(w, "ctx", 4) for w in near]
     take = flip(give, "tp", 2)
-
-    def part_of(value, j):
-        starts = [k * channels + j * width for k in range(2)]
-        return jnp.concatenate([value[:, at : at + width] for at in starts], axis=1)
-
-    take_z = [flip(part_of(take, j), "ctx", 4) for j in range(chunks)]
+    near_x = [flip(w, "ctx", 1) for w in near]
+    take_z = [flip(take[:, 2 * j * width : 2 * (j + 1) * width], "ctx", 4) for j in range(chunks)]
     take_x = flip(take, "ctx", 1)
     near_zx = [flip(w, "ctx", 1) for w in near_z]
     take_zx = [flip(take_z[j], "ctx", 1) for j in range(chunks)]
@@ -392,8 +399,10 @@
     rows = residual.shape[0]
     outs = []
     for j in range(chunks):
-        weights = [(w, False) for w in (near, take, *near_x, take_x, *near_z)]
-        weights += [(take_z[j], True)] + [(w, False) for w in near_zx] + [(take_zx[j], True)]
+        weights = [(w, CORE_FIRST) for w in near] + [(take, PART_FIRST)]
+        weights += [(w, CORE_FIRST) for w in near_x] + [(take_x, PART_FIRST)]
+        weights += [(w, CORE_FIRST) for w in near_z] + [(take_z[j], ONE_PART)]
+        weights += [(w, CORE_FIRST) for w in near_zx] + [(take_zx[j], ONE_PART)]
         theirs, ours = cube_product(flags, gated, weights, piece, width, j)
         total = ours + flip(theirs, "tp", 1).astype(jnp.float32)
         pair = flip(total[rows:].astype(jnp.bfloat16), "ctx", 2)

time: 122 us -> 121 us (level)
  local copies, waits for them, and re-layouts: 9.53 us -> 4.14 us
  starting transfers between devices: 34.4 us -> 36.5 us
  other arithmetic: 2.59 us -> 4.69 us
  waiting for transfers between devices: 61.3 us -> 59.2 us
  Pallas kernels: 13.9 us -> 15.6 us
    unnamed x26 -> x14, local copies, waits for them, and re-layouts: 7.13 us -> 1.86 us
    ppermute x3, waiting for transfers between devices: 4.77 us -> 0.01 us  [move(): return lax.ppermute(value, ('ctx', 'tp'), pairs)]
    ppermute x21, waiting for transfers between devices: 55.2 us -> 59.2 us  [flip(): return lax.ppermute(value, axis, [(i, i ^ bit) for i in range(count)])]
    ppermute x21, starting transfers between devices: 23.9 us -> 26.7 us  [flip(): return lax.ppermute(value, axis, [(i, i ^ bit) for i in range(count)])]
    select_n x1 -> x3, other arithmetic: 0.87 us -> 3.07 us  [the longest x2 2.15 us: project_cube(): jnp.where(y == 0, sides[0][lo:hi], sides[1][lo:hi])]
    pallas_call x5, Pallas kernels: 13.9 us -> 15.6 us  [in_vmem(): pl.pallas_call(kernel, out_shape=out_shape, in_specs=specs, out_specs=pl....]
    ppermute x1, waiting for transfers between devices: 1.38 us -> 0.01 us  [gated_blocks(): lax.ppermute(features[tok_rows - (filter_len - 1):], 'ctx', [(i, i + 1) f...]
  transfers between devices with their start and end apart: 25 -> 25, of which waited for: 13 -> 10; matrix products, arithmetic and copies ran while one was open for 3% -> 4% of each run, Pallas kernels for 9% -> 13%
where the time goes in v1:
time: 121 us; the launch traced here: 120 us
  waiting for transfers between devices  59.2 us (49%)
  starting transfers between devices  36.5 us (30%)
  Pallas kernels  15.6 us (13%)
  other arithmetic  4.69 us (4%)
  local copies, waits for them, and re-layouts  4.14 us (3%)
    ppermute x21, waiting for transfers between devices, flip(): return lax.ppermute(value, axis, [(i, i ^ bit) for i in range(count)])  59.2 us
    ppermute x21, starting transfers between devices, flip(): return lax.ppermute(value, axis, [(i, i ^ bit) for i in range(count)])  26.7 us
    pallas_call x5, Pallas kernels, in_vmem(): pl.pallas_call(kernel, out_shape=out_shape, in_specs=specs, out_specs=pl....  15.6 us
    ppermute x3, starting transfers between devices, move(): return lax.ppermute(value, ('ctx', 'tp'), pairs)  4.93 us
    ppermute x1, starting transfers between devices, gated_blocks(): lax.ppermute(features[tok_rows - (filter_len - 1):], 'ctx', [(i, i + 1) f...  4.87 us
  transfers between devices with their start and end apart: 25, of which 10 were waited for; matrix products, arithmetic and copies ran while one was open for 4% of the time, Pallas kernels for 13%

profile of v1, /device:TPU:0, one launch (start us, length us, event | category | flops | bytes accessed | tf_op | source)
XLA Modules:
  0.0 120.5 jit_solution(18329427704529037160)
XLA Ops:
  0.8 4.9 %collective-permute-start = (bf16[2,3,1024]{2,0,1:T(2,128)(2,1)S(1)}, bf16[2,3,1024]{2,0,1:T(2,128)(2,1)S(1)}, u32[]{:S(2)}, u32[]{:S(2)}) collective-permute-start(bf16[2,3,1024]{2,0,1:T(2,128)(2,1)S(1)} %slice.80), channel_id=1, source_target_pairs={{0,4},{4,8},{8,12},{12,16},{16,20},{20,24},{24,28},{1,5},{5,9},{9,... | collective-permute-start | bytes 36872 | tf_op jit(solution)/shard_map/ppermute | solution.py:239
  10.7 2.7 %collective-permute-start.14 = (bf16[80,2048]{1,0:T(8,128)(2,1)S(1)}, bf16[80,2048]{1,0:T(8,128)(2,1)S(1)}, u32[]{:S(2)}, u32[]{:S(2)}) collective-permute-start(bf16[80,2048]{1,0:T(8,128)(2,1)S(1)} %slice_select_fusion.refs_1_), channel_id=1, source_target_pairs={{0,16},{4,20},{8,24},{12,28},{16,0},{20,4},{24,8},{28,12},{1,17},{... | collective-permute-start | bytes 983048 | tf_op jit(solution)/shard_map/ppermute | solution.py:193
  13.3 3.0 %shard_map.64 = (f32[16,1024]{1,0:T(8,128)S(1)}, f32[16,8,1024]{2,1,0:T(8,128)S(1)}) custom-call(bf16[3,256,1024]{2,1,0:T(8,128)(2,1)S(1)} %bitcast.6, bf16[3,2,1024]{2,1,0:T(2,128)(2,1)S(1)} %bitcast.8, f32[3,3,1024]{2,1,0:T(4,128)S(1)} %copy-done.3, f32[16,1024]{1,0:T(8,128)S(1)} %copy-done), custom_call_target="tpu_custom_call" | custom-call | flops 1677721600 | bytes 8388608 | tf_op jit(solution)/shard_map/pallas_call | solution.py:220
  23.2 2.8 %collective-permute-done.2 = f32[16,1024]{1,0:T(8,128)S(1)} collective-permute-done((f32[16,1024]{1,0:T(8,128)S(1)}, f32[16,1024]{1,0:T(8,128)S(1)}, u32[]{:S(2)}, u32[]{:S(2)}) %collective-permute-start.2) | collective-permute-done | bytes 65568 | tf_op jit(solution)/shard_map/ppermute | solution.py:193
  26.0 2.1 %collective-permute-start.3 = (f32[16,1024]{1,0:T(8,128)S(1)}, f32[16,1024]{1,0:T(8,128)S(1)}, u32[]{:S(2)}, u32[]{:S(2)}) collective-permute-start(f32[16,1024]{1,0:T(8,128)S(1)} %select_add_fusion.1), channel_id=1, source_target_pairs={{0,16},{4,20},{8,24},{12,28},{16,0},{20,4},{24,8},{28,12},{1,17},{... | collective-permute-start | bytes 196616 | tf_op jit(solution)/shard_map/ppermute | solution.py:193
  29.1 5.0 %shard_map.65 = (f32[32,8,1024]{2,1,0:T(8,128)S(1)}, f32[32,8,1024]{2,1,0:T(8,128)S(1)}) custom-call(bf16[3,256,1024]{2,1,0:T(8,128)(2,1)S(1)} %bitcast.7, bf16[3,2,1024]{2,1,0:T(2,128)(2,1)S(1)} %bitcast.9, f32[3,3,1024]{2,1,0:T(4,128)S(1)} %copy-done.3, f32[16,1024]{1,0:T(8,128)S(1)} %copy-done, f32[16,1024]{1,0:T(8,128)S(1)} %copy-done.2, ...), custom_call_target="tpu_custom_call" | custom-call | flops 1677721600 | bytes 8388608 | tf_op jit(solution)/shard_map/pallas_call | solution.py:220
  34.1 4.7 %collective-permute-done.3 = f32[16,1024]{1,0:T(8,128)S(1)} collective-permute-done((f32[16,1024]{1,0:T(8,128)S(1)}, f32[16,1024]{1,0:T(8,128)S(1)}, u32[]{:S(2)}, u32[]{:S(2)}) %collective-permute-start.3) | collective-permute-done | bytes 65568 | tf_op jit(solution)/shard_map/ppermute | solution.py:193
  38.8 2.3 %shard_map.66 = (bf16[256,512]{1,0:T(8,128)(2,1)S(1)}, bf16[256,512]{1,0:T(8,128)(2,1)S(1)}) custom-call(s32[4]{0:T(128)S(1)} %pad_add_fusion.flags, f32[16,1024]{1,0:T(8,128)S(1)} %copy-done, f32[16,1024]{1,0:T(8,128)S(1)} %copy-done.2, f32[32,8,1024]{2,1,0:T(8,128)S(1)} %get-tuple-element.16.gate, f32[32,8,1024]{2,1,0:T(8,128)S(1)} %get-tuple-element.17.local, ...), custom_call_target="tpu_custom_call" | custom-call | flops 1677721600 | bytes 8388608 | tf_op jit(solution)/shard_map/pallas_call | solution.py:220
  42.4 3.0 %collective-permute-start.4 = (bf16[256,512]{1,0:T(8,128)(2,1)S(1)}, bf16[256,512]{1,0:T(8,128)(2,1)S(1)}, u32[]{:S(2)}, u32[]{:S(2)}) collective-permute-start(bf16[256,512]{1,0:T(8,128)(2,1)S(1)} %get-tuple-element.20), channel_id=1, source_target_pairs={{0,1},{2,3},{4,5},{6,7},{9,8},{11,10},{13,12},{15,14},{16,17},{18,... | collective-permute-start | bytes 786440 | tf_op jit(solution)/shard_map/ppermute | solution.py:388
  46.2 5.4 %collective-permute-done.10.refs_3_ = bf16[48,2048]{1,0:T(8,128)(2,1)S(1)} collective-permute-done((bf16[48,2048]{1,0:T(8,128)(2,1)S(1)}, bf16[48,2048]{1,0:T(8,128)(2,1)S(1)}, u32[]{:S(2)}, u32[]{:S(2)}) %collective-permute-start.10) | collective-permute-done | bytes 196640 | tf_op jit(solution)/shard_map/ppermute | solution.py:193
  51.9 1.7 %collective-permute-start.17 = (bf16[80,2048]{1,0:T(8,128)(2,1)S(1)}, bf16[80,2048]{1,0:T(8,128)(2,1)S(1)}, u32[]{:S(2)}, u32[]{:S(2)}) collective-permute-start(bf16[80,2048]{1,0:T(8,128)(2,1)S(1)} %collective-permute-done.14.refs_7_), channel_id=1, source_target_pairs={{0,4},{4,0},{8,12},{12,8},{16,20},{20,16},{24,28},{28,24},{1,5},{5... | collective-permute-start | bytes 983048 | tf_op jit(solution)/shard_map/ppermute | solution.py:193
  53.6 3.4 %collective-permute-start.21 = (bf16[128,1024]{1,0:T(8,128)(2,1)S(1)}, bf16[128,1024]{1,0:T(8,128)(2,1)S(1)}, u32[]{:S(2)}, u32[]{:S(2)}) collective-permute-start(bf16[128,1024]{1,0:T(8,128)(2,1)S(1)} %get-tuple-element.36), channel_id=1, source_target_pairs={{0,16},{4,20},{8,24},{12,28},{16,0},{20,4},{24,8},{28,12},{1,17},{... | collective-permute-start | bytes 786440 | tf_op jit(solution)/shard_map/ppermute | solution.py:193
  57.4 1.8 %collective-permute-start.16 = (bf16[48,2048]{1,0:T(8,128)(2,1)S(1)}, bf16[48,2048]{1,0:T(8,128)(2,1)S(1)}, u32[]{:S(2)}, u32[]{:S(2)}) collective-permute-start(bf16[48,2048]{1,0:T(8,128)(2,1)S(1)} %collective-permute-done.13.refs_6_), channel_id=1, source_target_pairs={{0,4},{4,0},{8,12},{12,8},{16,20},{20,16},{24,28},{28,24},{1,5},{5... | collective-permute-start | bytes 589832 | tf_op jit(solution)/shard_map/ppermute | solution.py:193
  59.2 3.0 %collective-permute-done.11.refs_4_ = bf16[80,2048]{1,0:T(8,128)(2,1)S(1)} collective-permute-done((bf16[80,2048]{1,0:T(8,128)(2,1)S(1)}, bf16[80,2048]{1,0:T(8,128)(2,1)S(1)}, u32[]{:S(2)}, u32[]{:S(2)}) %collective-permute-start.11) | collective-permute-done | bytes 327712 | tf_op jit(solution)/shard_map/ppermute | solution.py:193
  62.7 19.5 %collective-permute-done.16.refs_9_ = bf16[48,2048]{1,0:T(8,128)(2,1)S(1)} collective-permute-done((bf16[48,2048]{1,0:T(8,128)(2,1)S(1)}, bf16[48,2048]{1,0:T(8,128)(2,1)S(1)}, u32[]{:S(2)}, u32[]{:S(2)}) %collective-permute-start.16) | collective-permute-done | bytes 196640 | tf_op jit(solution)/shard_map/ppermute | solution.py:193
  82.2 3.4 %collective-permute-start.15 = (bf16[128,1024]{1,0:T(8,128)(2,1)S(1)}, bf16[128,1024]{1,0:T(8,128)(2,1)S(1)}, u32[]{:S(2)}, u32[]{:S(2)}) collective-permute-start(bf16[128,1024]{1,0:T(8,128)(2,1)S(1)} %get-tuple-element.35), channel_id=1, source_target_pairs={{0,16},{4,20},{8,24},{12,28},{16,0},{20,4},{24,8},{28,12},{1,17},{... | collective-permute-start | bytes 786440 | tf_op jit(solution)/shard_map/ppermute | solution.py:193
  86.7 8.9 %collective-permute-done.15.refs_8_ = bf16[128,1024]{1,0:T(8,128)(2,1)S(1)} collective-permute-done((bf16[128,1024]{1,0:T(8,128)(2,1)S(1)}, bf16[128,1024]{1,0:T(8,128)(2,1)S(1)}, u32[]{:S(2)}, u32[]{:S(2)}) %collective-permute-start.15) | collective-permute-done | bytes 262176 | tf_op jit(solution)/shard_map/ppermute | solution.py:193
  96.2 2.7 %shard_map.68 = (bf16[512,512]{1,0:T(8,128)(2,1)S(1)}, f32[512,512]{1,0:T(8,128)S(1)}) custom-call(s32[4]{0:T(128)S(1)} %pad_add_fusion.flags, bf16[256,512]{1,0:T(8,128)(2,1)S(1)} %broadcast_select_fusion.1.own_c, bf16[256,512]{1,0:T(8,128)(2,1)S(1)} %broadcast_select_fusion.own_o, bf16[256,512]{1,0:T(8,128)(2,1)S(1)} %collective-permute-done.7.other_c, ...), custom_call_target="tpu_custom_call" | custom-call | flops 1073741824 | bytes 5368709 | tf_op jit(solution)/shard_map/pallas_call | solution.py:220
  99.0 3.0 %collective-permute-done.18.refs_11_ = bf16[128,1024]{1,0:T(8,128)(2,1)S(1)} collective-permute-done((bf16[128,1024]{1,0:T(8,128)(2,1)S(1)}, bf16[128,1024]{1,0:T(8,128)(2,1)S(1)}, u32[]{:S(2)}, u32[]{:S(2)}) %collective-permute-start.18) | collective-permute-done | bytes 262176 | tf_op jit(solution)/shard_map/ppermute | solution.py:193
  101.9 2.7 %shard_map.67 = (bf16[512,512]{1,0:T(8,128)(2,1)S(1)}, f32[512,512]{1,0:T(8,128)S(1)}) custom-call(s32[4]{0:T(128)S(1)} %pad_add_fusion.flags, bf16[256,512]{1,0:T(8,128)(2,1)S(1)} %broadcast_select_fusion.1.own_c, bf16[256,512]{1,0:T(8,128)(2,1)S(1)} %broadcast_select_fusion.own_o, bf16[256,512]{1,0:T(8,128)(2,1)S(1)} %collective-permute-done.7.other_c, ...), custom_call_target="tpu_custom_call" | custom-call | flops 1073741824 | bytes 5368709 | tf_op jit(solution)/shard_map/pallas_call | solution.py:220
  104.9 1.9 %collective-permute-start.24 = (bf16[256,512]{1,0:T(8,128)(2,1)S(1)}, bf16[256,512]{1,0:T(8,128)(2,1)S(1)}, u32[]{:S(2)}, u32[]{:S(2)}) collective-permute-start(bf16[256,512]{1,0:T(8,128)(2,1)S(1)} %slice.124), channel_id=1, source_target_pairs={{0,8},{4,12},{8,0},{12,4},{16,24},{20,28},{24,16},{28,20},{1,9},{5... | collective-permute-start | bytes 786440 | tf_op jit(solution)/shard_map/ppermute | solution.py:193
  107.0 1.7 %collective-permute-start.20 = (bf16[256,512]{1,0:T(8,128)(2,1)S(1)}, bf16[256,512]{1,0:T(8,128)(2,1)S(1)}, u32[]{:S(2)}, u32[]{:S(2)}) collective-permute-start(bf16[256,512]{1,0:T(8,128)(2,1)S(1)} %slice.125), channel_id=1, source_target_pairs={{0,8},{4,12},{8,0},{12,4},{16,24},{20,28},{24,16},{28,20},{1,9},{5... | collective-permute-start | bytes 786440 | tf_op jit(solution)/shard_map/ppermute | solution.py:193
  108.7 5.4 %collective-permute-done.24 = bf16[256,512]{1,0:T(8,128)(2,1)S(1)} collective-permute-done((bf16[256,512]{1,0:T(8,128)(2,1)S(1)}, bf16[256,512]{1,0:T(8,128)(2,1)S(1)}, u32[]{:S(2)}, u32[]{:S(2)}) %collective-permute-start.24) | collective-permute-done | bytes 262176 | tf_op jit(solution)/shard_map/ppermute | solution.py:193
  114.1 5.2 %collective-permute-done.20 = bf16[256,512]{1,0:T(8,128)(2,1)S(1)} collective-permute-done((bf16[256,512]{1,0:T(8,128)(2,1)S(1)}, bf16[256,512]{1,0:T(8,128)(2,1)S(1)}, u32[]{:S(2)}, u32[]{:S(2)}) %collective-permute-start.20) | collective-permute-done | bytes 262176 | tf_op jit(solution)/shard_map/ppermute | solution.py:193
  (63 shorter events, 20.2 us)
Async XLA Ops:
  0.8 12.5 %collective-permute-start = (bf16[2,3,1024]{2,0,1:T(2,128)(2,1)S(1)}, bf16[2,3,1024]{2,0,1:T(2,128)(2,1)S(1)}, u32[]{:S(2)}, u32[]{:S(2)}) collective-permute-start(bf16[2,3,1024]{2,0,1:T(2,128)(2,1)S(1)} %slice.80), channel_id=1, source_target_pairs={{0,4},{4,8},{8,12},{12,16},{16,20},{20,24},{24,28},{1,5},{5,9},{9,... | collective-permute-start | bytes 36872 | tf_op jit(solution)/shard_map/ppermute | solution.py:239
  8.0 37.4 %collective-permute-start.9 = (bf16[128,2048]{1,0:T(8,128)(2,1)}, bf16[128,2048]{1,0:T(8,128)(2,1)S(1)}, u32[]{:S(2)}, u32[]{:S(2)}) collective-permute-start(bf16[128,2048]{1,0:T(8,128)(2,1)} %maximum_select_fusion), channel_id=1, source_target_pairs={{0,2},{1,3},{2,0},{3,1},{4,6},{5,7},{6,4},{7,5},{8,10},{9,11},{10,... | collective-permute-start | bytes 1572872 | tf_op jit(solution)/shard_map/ppermute | solution.py:193
  10.7 41.2 %collective-permute-start.14 = (bf16[80,2048]{1,0:T(8,128)(2,1)S(1)}, bf16[80,2048]{1,0:T(8,128)(2,1)S(1)}, u32[]{:S(2)}, u32[]{:S(2)}) collective-permute-start(bf16[80,2048]{1,0:T(8,128)(2,1)S(1)} %slice_select_fusion.refs_1_), channel_id=1, source_target_pairs={{0,16},{4,20},{8,24},{12,28},{16,0},{20,4},{24,8},{28,12},{1,17},{... | collective-permute-start | bytes 983048 | tf_op jit(solution)/shard_map/ppermute | solution.py:193
  17.2 4.3 %collective-permute-start.1 = (f32[16,1024]{1,0:T(8,128)S(1)}, f32[16,1024]{1,0:T(8,128)S(1)}, u32[]{:S(2)}, u32[]{:S(2)}) collective-permute-start(f32[16,1024]{1,0:T(8,128)S(1)} %get-tuple-element.18), channel_id=1, source_target_pairs={{0,4},{4,0},{8,12},{12,8},{16,20},{20,16},{24,28},{28,24},{1,5},{5... | collective-permute-start | bytes 196616 | tf_op jit(solution)/shard_map/ppermute | solution.py:193
  19.8 25.6 %collective-permute-start.13 = (bf16[48,2048]{1,0:T(8,128)(2,1)S(1)}, bf16[48,2048]{1,0:T(8,128)(2,1)S(1)}, u32[]{:S(2)}, u32[]{:S(2)}) collective-permute-start(bf16[48,2048]{1,0:T(8,128)(2,1)S(1)} %slice_select_fusion.1.refs_0_), channel_id=1, source_target_pairs={{0,16},{4,20},{8,24},{12,28},{16,0},{20,4},{24,8},{28,12},{1,17},{... | collective-permute-start | bytes 589832 | tf_op jit(solution)/shard_map/ppermute | solution.py:193
  21.5 4.5 %collective-permute-start.2 = (f32[16,1024]{1,0:T(8,128)S(1)}, f32[16,1024]{1,0:T(8,128)S(1)}, u32[]{:S(2)}, u32[]{:S(2)}) collective-permute-start(f32[16,1024]{1,0:T(8,128)S(1)} %select_add_fusion.2), channel_id=1, source_target_pairs={{0,8},{4,12},{8,0},{12,4},{16,24},{20,28},{24,16},{28,20},{1,9},{5... | collective-permute-start | bytes 196616 | tf_op jit(solution)/shard_map/ppermute | solution.py:193
  26.0 12.8 %collective-permute-start.3 = (f32[16,1024]{1,0:T(8,128)S(1)}, f32[16,1024]{1,0:T(8,128)S(1)}, u32[]{:S(2)}, u32[]{:S(2)}) collective-permute-start(f32[16,1024]{1,0:T(8,128)S(1)} %select_add_fusion.1), channel_id=1, source_target_pairs={{0,16},{4,20},{8,24},{12,28},{16,0},{20,4},{24,8},{28,12},{1,17},{... | collective-permute-start | bytes 196616 | tf_op jit(solution)/shard_map/ppermute | solution.py:193
  41.1 12.6 %collective-permute-start.5 = (bf16[256,512]{1,0:T(8,128)(2,1)S(1)}, bf16[256,512]{1,0:T(8,128)(2,1)S(1)}, u32[]{:S(2)}, u32[]{:S(2)}) collective-permute-start(bf16[256,512]{1,0:T(8,128)(2,1)S(1)} %get-tuple-element.19), channel_id=1, source_target_pairs={{1,9},{3,11},{5,13},{7,15},{8,0},{10,2},{12,4},{14,6},{17,25},{19,... | collective-permute-start | bytes 786440 | tf_op jit(solution)/shard_map/ppermute | solution.py:388
  42.4 14.6 %collective-permute-start.4 = (bf16[256,512]{1,0:T(8,128)(2,1)S(1)}, bf16[256,512]{1,0:T(8,128)(2,1)S(1)}, u32[]{:S(2)}, u32[]{:S(2)}) collective-permute-start(bf16[256,512]{1,0:T(8,128)(2,1)S(1)} %get-tuple-element.20), channel_id=1, source_target_pairs={{0,1},{2,3},{4,5},{6,7},{9,8},{11,10},{13,12},{15,14},{16,17},{18,... | collective-permute-start | bytes 786440 | tf_op jit(solution)/shard_map/ppermute | solution.py:388
  45.4 6.2 %collective-permute-start.10 = (bf16[48,2048]{1,0:T(8,128)(2,1)S(1)}, bf16[48,2048]{1,0:T(8,128)(2,1)S(1)}, u32[]{:S(2)}, u32[]{:S(2)}) collective-permute-start(bf16[48,2048]{1,0:T(8,128)(2,1)S(1)} %slice_select_fusion.1.refs_0_), channel_id=1, source_target_pairs={{0,4},{4,0},{8,12},{12,8},{16,20},{20,16},{24,28},{28,24},{1,5},{5... | collective-permute-start | bytes 589832 | tf_op jit(solution)/shard_map/ppermute | solution.py:193
  45.5 11.9 %collective-permute-start.6 = (bf16[256,512]{1,0:T(8,128)(2,1)S(1)}, bf16[256,512]{1,0:T(8,128)(2,1)S(1)}, u32[]{:S(2)}, u32[]{:S(2)}) collective-permute-start(bf16[256,512]{1,0:T(8,128)(2,1)S(1)} %get-tuple-element.20), channel_id=1, source_target_pairs={{1,8},{3,10},{5,12},{7,14},{8,1},{10,3},{12,5},{14,7},{17,24},{19,... | collective-permute-start | bytes 786440 | tf_op jit(solution)/shard_map/ppermute | solution.py:388
  51.6 10.6 %collective-permute-start.11 = (bf16[80,2048]{1,0:T(8,128)(2,1)S(1)}, bf16[80,2048]{1,0:T(8,128)(2,1)S(1)}, u32[]{:S(2)}, u32[]{:S(2)}) collective-permute-start(bf16[80,2048]{1,0:T(8,128)(2,1)S(1)} %slice_select_fusion.refs_1_), channel_id=1, source_target_pairs={{0,4},{4,0},{8,12},{12,8},{16,20},{20,16},{24,28},{28,24},{1,5},{5... | collective-permute-start | bytes 983048 | tf_op jit(solution)/shard_map/ppermute | solution.py:193
  51.9 33.7 %collective-permute-start.17 = (bf16[80,2048]{1,0:T(8,128)(2,1)S(1)}, bf16[80,2048]{1,0:T(8,128)(2,1)S(1)}, u32[]{:S(2)}, u32[]{:S(2)}) collective-permute-start(bf16[80,2048]{1,0:T(8,128)(2,1)S(1)} %collective-permute-done.14.refs_7_), channel_id=1, source_target_pairs={{0,4},{4,0},{8,12},{12,8},{16,20},{20,16},{24,28},{28,24},{1,5},{5... | collective-permute-start | bytes 983048 | tf_op jit(solution)/shard_map/ppermute | solution.py:193
  53.6 32.5 %collective-permute-start.21 = (bf16[128,1024]{1,0:T(8,128)(2,1)S(1)}, bf16[128,1024]{1,0:T(8,128)(2,1)S(1)}, u32[]{:S(2)}, u32[]{:S(2)}) collective-permute-start(bf16[128,1024]{1,0:T(8,128)(2,1)S(1)} %get-tuple-element.36), channel_id=1, source_target_pairs={{0,16},{4,20},{8,24},{12,28},{16,0},{20,4},{24,8},{28,12},{1,17},{... | collective-permute-start | bytes 786440 | tf_op jit(solution)/shard_map/ppermute | solution.py:193
  57.0 39.2 %collective-permute-start.12 = (bf16[128,2048]{1,0:T(8,128)(2,1)S(1)}, bf16[128,2048]{1,0:T(8,128)(2,1)S(1)}, u32[]{:S(2)}, u32[]{:S(2)}) collective-permute-start(bf16[128,2048]{1,0:T(8,128)(2,1)S(1)} %collective-permute-done.9.refs_2_), channel_id=1, source_target_pairs={{0,4},{4,0},{8,12},{12,8},{16,20},{20,16},{24,28},{28,24},{1,5},{5... | collective-permute-start | bytes 1572872 | tf_op jit(solution)/shard_map/ppermute | solution.py:193
  57.4 24.9 %collective-permute-start.16 = (bf16[48,2048]{1,0:T(8,128)(2,1)S(1)}, bf16[48,2048]{1,0:T(8,128)(2,1)S(1)}, u32[]{:S(2)}, u32[]{:S(2)}) collective-permute-start(bf16[48,2048]{1,0:T(8,128)(2,1)S(1)} %collective-permute-done.13.refs_6_), channel_id=1, source_target_pairs={{0,4},{4,0},{8,12},{12,8},{16,20},{20,16},{24,28},{28,24},{1,5},{5... | collective-permute-start | bytes 589832 | tf_op jit(solution)/shard_map/ppermute | solution.py:193
  62.2 34.0 %collective-permute-start.8 = (bf16[256,512]{1,0:T(8,128)(2,1)S(1)}, bf16[256,512]{1,0:T(8,128)(2,1)S(1)}, u32[]{:S(2)}, u32[]{:S(2)}) collective-permute-start(bf16[256,512]{1,0:T(8,128)(2,1)S(1)} %broadcast_select_fusion.own_o), channel_id=1, source_target_pairs={{0,2},{1,3},{2,0},{3,1},{4,6},{5,7},{6,4},{7,5},{8,10},{9,11},{10,... | collective-permute-start | bytes 786440 | tf_op jit(solution)/shard_map/ppermute | solution.py:193
  82.2 13.3 %collective-permute-start.15 = (bf16[128,1024]{1,0:T(8,128)(2,1)S(1)}, bf16[128,1024]{1,0:T(8,128)(2,1)S(1)}, u32[]{:S(2)}, u32[]{:S(2)}) collective-permute-start(bf16[128,1024]{1,0:T(8,128)(2,1)S(1)} %get-tuple-element.35), channel_id=1, source_target_pairs={{0,16},{4,20},{8,24},{12,28},{16,0},{20,4},{24,8},{28,12},{1,17},{... | collective-permute-start | bytes 786440 | tf_op jit(solution)/shard_map/ppermute | solution.py:193
  85.6 10.6 %collective-permute-start.7 = (bf16[256,512]{1,0:T(8,128)(2,1)S(1)}, bf16[256,512]{1,0:T(8,128)(2,1)S(1)}, u32[]{:S(2)}, u32[]{:S(2)}) collective-permute-start(bf16[256,512]{1,0:T(8,128)(2,1)S(1)} %broadcast_select_fusion.1.own_c), channel_id=1, source_target_pairs={{0,2},{1,3},{2,0},{3,1},{4,6},{5,7},{6,4},{7,5},{8,10},{9,11},{10,... | collective-permute-start | bytes 786440 | tf_op jit(solution)/shard_map/ppermute | solution.py:193
  86.1 10.1 %collective-permute-start.22 = (bf16[128,1024]{1,0:T(8,128)(2,1)S(1)}, bf16[128,1024]{1,0:T(8,128)(2,1)S(1)}, u32[]{:S(2)}, u32[]{:S(2)}) collective-permute-start(bf16[128,1024]{1,0:T(8,128)(2,1)S(1)} %collective-permute-done.21.refs_8_), channel_id=1, source_target_pairs={{0,4},{4,0},{8,12},{12,8},{16,20},{20,16},{24,28},{28,24},{1,5},{5... | collective-permute-start | bytes 786440 | tf_op jit(solution)/shard_map/ppermute | solution.py:193
  95.6 6.4 %collective-permute-start.18 = (bf16[128,1024]{1,0:T(8,128)(2,1)S(1)}, bf16[128,1024]{1,0:T(8,128)(2,1)S(1)}, u32[]{:S(2)}, u32[]{:S(2)}) collective-permute-start(bf16[128,1024]{1,0:T(8,128)(2,1)S(1)} %collective-permute-done.15.refs_8_), channel_id=1, source_target_pairs={{0,4},{4,0},{8,12},{12,8},{16,20},{20,16},{24,28},{28,24},{1,5},{5... | collective-permute-start | bytes 786440 | tf_op jit(solution)/shard_map/ppermute | solution.py:193
  98.9 5.8 %collective-permute-start.23 = (bf16[512,512]{1,0:T(8,128)(2,1)S(1)}, bf16[512,512]{1,0:T(8,128)(2,1)S(1)}, u32[]{:S(2)}, u32[]{:S(2)}) collective-permute-start(bf16[512,512]{1,0:T(8,128)(2,1)S(1)} %get-tuple-element.24), channel_id=1, source_target_pairs={{0,1},{1,0},{2,3},{3,2},{4,5},{5,4},{6,7},{7,6},{8,9},{9,8},{10,11... | collective-permute-start | bytes 1572872 | tf_op jit(solution)/shard_map/ppermute | solution.py:193
  104.9 9.2 %collective-permute-start.24 = (bf16[256,512]{1,0:T(8,128)(2,1)S(1)}, bf16[256,512]{1,0:T(8,128)(2,1)S(1)}, u32[]{:S(2)}, u32[]{:S(2)}) collective-permute-start(bf16[256,512]{1,0:T(8,128)(2,1)S(1)} %slice.124), channel_id=1, source_target_pairs={{0,8},{4,12},{8,0},{12,4},{16,24},{20,28},{24,16},{28,20},{1,9},{5... | collective-permute-start | bytes 786440 | tf_op jit(solution)/shard_map/ppermute | solution.py:193
  107.0 12.4 %collective-permute-start.20 = (bf16[256,512]{1,0:T(8,128)(2,1)S(1)}, bf16[256,512]{1,0:T(8,128)(2,1)S(1)}, u32[]{:S(2)}, u32[]{:S(2)}) collective-permute-start(bf16[256,512]{1,0:T(8,128)(2,1)S(1)} %slice.125), channel_id=1, source_target_pairs={{0,8},{4,12},{8,0},{12,4},{16,24},{20,28},{24,16},{28,20},{1,9},{5... | collective-permute-start | bytes 786440 | tf_op jit(solution)/shard_map/ppermute | solution.py:193
  (8 other events, 50.1 us)

commit v2 on v1

--- a/solution.py
+++ b/solution.py
@@ -176,7 +176,7 @@
         lax.fori_loop(0, seg_len, one_token, terms, unroll=UNROLL)
         place = pl.ds(pl.multiple_of((group // parts) * LANES, LANES), LANES)
         value = rows[...].astype(jnp.bfloat16)
-        turned = jnp.bitwise_xor(lax.rem(group, parts), flags[0] if parts > 1 else 0)
+        turned = jnp.bitwise_xor(lax.rem(group, parts), flags[4] if parts > 1 else 0)
         for k in range(parts):
 
             @pl.when(turned == k)
@@ -196,19 +196,23 @@
 def entering_state(end, log_decay, tok_rows):
     place = lax.axis_index("ctx")
     count = lax.axis_size("ctx")
+    decay_over = lambda tokens: jnp.exp(-log_decay * tokens)
     prefix = jnp.zeros_like(end)
     total = end
-    bit = 1
+    bit = 2
     while bit < count:
         other = flip(total, "ctx", bit)
         upper = (place & bit) != 0
-        covered = (place & (bit - 1)).astype(jnp.float32) * float(tok_rows)
-        prefix = prefix + jnp.where(upper, jnp.exp(-log_decay * covered) * other, 0.0)
+        covered = (place & (bit - 2)).astype(jnp.float32) * float(tok_rows)
+        prefix = prefix + jnp.where(upper, decay_over(covered) * other, 0.0)
         first = jnp.where(upper, other, total)
         second = jnp.where(upper, total, other)
-        total = jnp.exp(-log_decay * float(tok_rows * bit)) * first + second
+        total = decay_over(float(tok_rows * bit)) * first + second
         bit *= 2
-    return prefix
+    even = (place & 1) == 0
+    message = jnp.where(even, decay_over(float(2 * tok_rows)) * prefix + end, prefix)
+    other = flip(message, "ctx", 1)
+    return decay_over(float(tok_rows)) * prefix + other
 
 
 def in_vmem(kernel, out_shape, inputs, scratch, flops, flags=None):
@@ -293,20 +297,21 @@
                     ]
 
 
-def cube_kernel(piece, orders, part, flags, own_c, own_o, other_c, other_o, *refs):
+def cube_kernel(piece, orders, part, flags, kept, from_q, from_r, from_1, from_2, *refs):
     weights, (theirs, mine, left) = refs[:-3], refs[-3:]
     width = mine.shape[1]
     full = weights[0].shape[1] // 2
     tile = min(width, 256)
-    own, other = (own_c, own_o), (other_c, other_o)
-
-    @pl.when(flags[3] == 1)
-    def _():
-        fill_left(left, flags, piece, own, other)
-
-    @pl.when(flags[3] == 0)
-    def _():
-        fill_left(left, flags, piece, other, own)
+
+    for stays, own, other in (
+        (1, (kept, from_q), (from_2, from_1)),
+        (0, (from_q, from_r), (from_1, from_2)),
+    ):
+        for same, near_plane, far_plane in ((1, own, other), (0, other, own)):
+
+            @pl.when(jnp.logical_and(flags[3] == same, flags[5] == stays))
+            def _(near_plane=near_plane, far_plane=far_plane):
+                fill_left(left, flags, piece, near_plane, far_plane)
 
     for side, out in ((1 - flags[0], theirs), (flags[0], mine)):
 
@@ -347,9 +352,9 @@
     return core, y, x, zp, zh
 
 
-def project_cube(mine, sib, flags, residual, out_weight, chunks):
+def project_cube(leaves, turns, flags, residual, out_weight, chunks):
     ctx, tp = lax.axis_size("ctx"), lax.axis_size("tp")
-    core, y, _, zp, _ = cube_place()
+    _, y, _, _, _ = cube_place()
     piece, columns = out_weight.shape
     channels = columns // tp
     width = channels // chunks
@@ -373,28 +378,30 @@
     near_zx = [flip(w, "ctx", 1) for w in near_z]
     take_zx = [flip(take_z[j], "ctx", 1) for j in range(chunks)]
 
-    stays = core == zp
-    pairs_1, pairs_2, pairs_3 = [], [], []
+    moves = {"gate_q": [], "gate_r": [], "gate_1": [], "gate_2": []}
     for ci in range(ctx):
         for ti in range(tp):
-            source = ci * tp + ti
+            source, over = ci * tp + ti, (ci ^ 2) * tp
             if (ti & 1) == ((ci >> 1) & 1):
-                pairs_1.append((source, ci * tp + (ti ^ 1)))
+                moves["gate_q"].append((source, ci * tp + (ti ^ 1)))
+                moves["gate_1"].append((source, ci * tp + (ti ^ 3)))
+                moves["gate_2"].append((source, ci * tp + (ti ^ 2)))
             else:
-                pairs_2.append((source, (ci ^ 2) * tp + ti))
-                pairs_3.append((source, (ci ^ 2) * tp + (ti ^ 1)))
-
-    def move(value, pairs):
-        return lax.ppermute(value, ("ctx", "tp"), pairs)
-
-    from_core = move(sib, pairs_1)
-    from_z = move(mine, pairs_2)
-    from_both = move(sib, pairs_3)
-    own_c = jnp.where(stays, mine, from_core)
-    own_o = jnp.where(stays, from_z, from_both)
-    other_c = flip(own_c, "tp", 2)
-    other_o = flip(own_o, "tp", 2)
-    gated = (own_c, own_o, other_c, other_o)
+                moves["gate_q"].append((source, over + ti))
+                moves["gate_r"].append((source, over + (ti ^ 1)))
+                moves["gate_1"].append((source, over + (ti ^ 2)))
+                moves["gate_2"].append((source, over + (ti ^ 3)))
+
+    def move(value, name):
+        return lax.ppermute(value, ("ctx", "tp"), moves[name])
+
+    gated = (
+        turns,
+        move(leaves, "gate_q"),
+        move(turns, "gate_r"),
+        move(leaves, "gate_1"),
+        move(turns, "gate_2"),
+    )
 
     rows = residual.shape[0]
     outs = []
@@ -415,10 +422,12 @@
     ctx, tp = lax.axis_size("ctx"), lax.axis_size("tp")
     piece = out_weight.shape[0]
     if cube_shaped(ctx, tp) and piece == LANES:
-        core, y, x, _, zh = cube_place()
-        flags = jnp.stack([core, x, y, (y == zh).astype(jnp.int32)]).astype(jnp.int32)
-        mine, sib = gated_blocks(features, short_filter, log_decay, residue, flags, 2)
-        return project_cube(mine, sib, flags, residual, out_weight, CHUNKS)
+        core, y, x, zp, zh = cube_place()
+        stays = (core == zp).astype(jnp.int32)
+        same = (y == zh).astype(jnp.int32)
+        flags = jnp.stack([core, x, y, same, core ^ stays, stays]).astype(jnp.int32)
+        leaves, turns = gated_blocks(features, short_filter, log_decay, residue, flags, 2)
+        return project_cube(leaves, turns, flags, residual, out_weight, CHUNKS)
     flags = jnp.zeros((1,), jnp.int32)
     (gated,) = gated_blocks(features, short_filter, log_decay, residue, flags, 1)
     return project_gathered(gated, residual, out_weight)

time: 121 us -> 108 us (0.89)
  waiting for transfers between devices: 59.2 us -> 39.8 us
  starting transfers between devices: 36.5 us -> 44 us
    ppermute x21 -> x19, waiting for transfers between devices: 59.2 us -> 30.6 us  [flip(): return lax.ppermute(value, axis, [(i, i ^ bit) for i in range(count)])]
    ppermute x21 -> x19, starting transfers between devices: 26.7 us -> 36.8 us  [flip(): return lax.ppermute(value, axis, [(i, i ^ bit) for i in range(count)])]
    ppermute x3 -> x4, waiting for transfers between devices: 0.01 us -> 6.91 us  [move(): return lax.ppermute(value, ('ctx', 'tp'), moves[name])]
    ppermute x1, starting transfers between devices: 4.87 us -> 2.44 us  [gated_blocks(): lax.ppermute(features[tok_rows - (filter_len - 1):], 'ctx', [(i, i + 1) f...]
    ppermute x1, waiting for transfers between devices: 0.01 us -> 2.32 us  [gated_blocks(): lax.ppermute(features[tok_rows - (filter_len - 1):], 'ctx', [(i, i + 1) f...]
    ppermute x3 -> x4, starting transfers between devices: 4.93 us -> 4.73 us  [move(): return lax.ppermute(value, ('ctx', 'tp'), moves[name])]
  transfers between devices with their start and end apart: 25 -> 24, of which waited for: 10 -> 12; matrix products, arithmetic and copies ran while one was open for 4% -> 4% of each run, Pallas kernels for 13% -> 15%
where the time goes in v2:
time: 108 us; the launch traced here: 107 us
  starting transfers between devices  44 us (41%)
  waiting for transfers between devices  39.8 us (37%)
  Pallas kernels  15.6 us (14%)
  other arithmetic  3.9 us (4%)
  local copies, waits for them, and re-layouts  3.79 us (4%)
    ppermute x19, starting transfers between devices, flip(): return lax.ppermute(value, axis, [(i, i ^ bit) for i in range(count)])  36.8 us
    ppermute x19, waiting for transfers between devices, flip(): return lax.ppermute(value, axis, [(i, i ^ bit) for i in range(count)])  30.6 us
    pallas_call x5, Pallas kernels, in_vmem(): pl.pallas_call(kernel, out_shape=out_shape, in_specs=specs, out_specs=pl....  15.6 us
    ppermute x4, waiting for transfers between devices, move(): return lax.ppermute(value, ('ctx', 'tp'), moves[name])  6.91 us
    ppermute x4, starting transfers between devices, move(): return lax.ppermute(value, ('ctx', 'tp'), moves[name])  4.73 us
    ppermute x1, starting transfers between devices, gated_blocks(): lax.ppermute(features[tok_rows - (filter_len - 1):], 'ctx', [(i, i + 1) f...  2.44 us
    ppermute x1, waiting for transfers between devices, gated_blocks(): lax.ppermute(features[tok_rows - (filter_len - 1):], 'ctx', [(i, i + 1) f...  2.32 us
    select_n x2, other arithmetic, project_cube(): jnp.where(y == 0, sides[0][lo:hi], sides[1][lo:hi])  2.27 us
  transfers between devices with their start and end apart: 24, of which 12 were waited for; matrix products, arithmetic and copies ran while one was open for 4% of the time, Pallas kernels for 15%

profile of v2, /device:TPU:0, one launch (start us, length us, event | category | flops | bytes accessed | tf_op | source)
XLA Modules:
  0.0 107.3 jit_solution(2160905489510444213)
XLA Ops:
  1.2 4.1 %collective-permute-start.13 = (bf16[80,2048]{1,0:T(8,128)(2,1)S(1)}, bf16[80,2048]{1,0:T(8,128)(2,1)S(1)}, u32[]{:S(2)}, u32[]{:S(2)}) collective-permute-start(bf16[80,2048]{1,0:T(8,128)(2,1)S(1)} %slice_select_fusion.refs_1_), channel_id=1, source_target_pairs={{0,16},{4,20},{8,24},{12,28},{16,0},{20,4},{24,8},{28,12},{1,17},{... | collective-permute-start | bytes 983048 | tf_op jit(solution)/shard_map/ppermute | solution.py:193
  7.7 2.4 %collective-permute-start = (bf16[2,3,1024]{2,0,1:T(2,128)(2,1)S(1)}, bf16[2,3,1024]{2,0,1:T(2,128)(2,1)S(1)}, u32[]{:S(2)}, u32[]{:S(2)}) collective-permute-start(bf16[2,3,1024]{2,0,1:T(2,128)(2,1)S(1)} %slice.80), channel_id=1, source_target_pairs={{0,4},{4,8},{8,12},{12,16},{16,20},{20,24},{24,28},{1,5},{5,9},{9,... | collective-permute-start | bytes 36872 | tf_op jit(solution)/shard_map/ppermute | solution.py:243
  11.5 2.3 %collective-permute-done = bf16[2,3,1024]{2,0,1:T(2,128)(2,1)S(1)} collective-permute-done((bf16[2,3,1024]{2,0,1:T(2,128)(2,1)S(1)}, bf16[2,3,1024]{2,0,1:T(2,128)(2,1)S(1)}, u32[]{:S(2)}, u32[]{:S(2)}) %collective-permute-start) | collective-permute-done | bytes 12320 | tf_op jit(solution)/shard_map/ppermute | solution.py:243
  13.8 3.0 %shard_map.64 = (f32[16,1024]{1,0:T(8,128)S(1)}, f32[16,8,1024]{2,1,0:T(8,128)S(1)}) custom-call(bf16[3,256,1024]{2,1,0:T(8,128)(2,1)S(1)} %bitcast.8, bf16[3,2,1024]{2,1,0:T(2,128)(2,1)S(1)} %bitcast.10, f32[3,3,1024]{2,1,0:T(4,128)S(1)} %copy-done.4, f32[16,1024]{1,0:T(8,128)S(1)} %copy-done), custom_call_target="tpu_custom_call" | custom-call | flops 1677721600 | bytes 8388608 | tf_op jit(solution)/shard_map/pallas_call | solution.py:224
  16.9 2.4 %collective-permute-start.1 = (f32[16,1024]{1,0:T(8,128)S(1)}, f32[16,1024]{1,0:T(8,128)S(1)}, u32[]{:S(2)}, u32[]{:S(2)}) collective-permute-start(f32[16,1024]{1,0:T(8,128)S(1)} %get-tuple-element.18), channel_id=1, source_target_pairs={{0,8},{4,12},{8,0},{12,4},{16,24},{20,28},{24,16},{28,20},{1,9},{5... | collective-permute-start | bytes 196616 | tf_op jit(solution)/shard_map/ppermute | solution.py:193
  21.6 9.9 %collective-permute-start.2 = (f32[16,1024]{1,0:T(8,128)S(1)}, f32[16,1024]{1,0:T(8,128)S(1)}, u32[]{:S(2)}, u32[]{:S(2)}) collective-permute-start(f32[16,1024]{1,0:T(8,128)S(1)} %select_add_fusion.1), channel_id=1, source_target_pairs={{0,16},{4,20},{8,24},{12,28},{16,0},{20,4},{24,8},{28,12},{1,17},{... | collective-permute-start | bytes 196616 | tf_op jit(solution)/shard_map/ppermute | solution.py:193
  34.0 5.0 %collective-permute-start.3 = (f32[16,1024]{1,0:T(8,128)S(1)}, f32[16,1024]{1,0:T(8,128)S(1)}, u32[]{:S(2)}, u32[]{:S(2)}) collective-permute-start(f32[16,1024]{1,0:T(8,128)S(1)} %add_select_fusion), channel_id=1, source_target_pairs={{0,4},{4,0},{8,12},{12,8},{16,20},{20,16},{24,28},{28,24},{1,5},{5... | collective-permute-start | bytes 196616 | tf_op jit(solution)/shard_map/ppermute | solution.py:193
  40.5 5.0 %shard_map.65 = (f32[32,8,1024]{2,1,0:T(8,128)S(1)}, f32[32,8,1024]{2,1,0:T(8,128)S(1)}) custom-call(bf16[3,256,1024]{2,1,0:T(8,128)(2,1)S(1)} %bitcast.9, bf16[3,2,1024]{2,1,0:T(2,128)(2,1)S(1)} %bitcast.11, f32[3,3,1024]{2,1,0:T(4,128)S(1)} %copy-done.4, f32[16,1024]{1,0:T(8,128)S(1)} %copy-done, f32[16,1024]{1,0:T(8,128)S(1)} %copy-done.3, ...), custom_call_target="tpu_custom_call" | custom-call | flops 1677721600 | bytes 8388608 | tf_op jit(solution)/shard_map/pallas_call | solution.py:224
  45.6 2.0 %collective-permute-start.15 = (bf16[48,2048]{1,0:T(8,128)(2,1)S(1)}, bf16[48,2048]{1,0:T(8,128)(2,1)S(1)}, u32[]{:S(2)}, u32[]{:S(2)}) collective-permute-start(bf16[48,2048]{1,0:T(8,128)(2,1)S(1)} %collective-permute-done.12.refs_6_), channel_id=1, source_target_pairs={{0,4},{4,0},{8,12},{12,8},{16,20},{20,16},{24,28},{28,24},{1,5},{5... | collective-permute-start | bytes 589832 | tf_op jit(solution)/shard_map/ppermute | solution.py:193
  47.6 2.3 %shard_map.66 = (bf16[256,512]{1,0:T(8,128)(2,1)S(1)}, bf16[256,512]{1,0:T(8,128)(2,1)S(1)}) custom-call(s32[6]{0:T(128)S(1)} %stack.31.flags, f32[16,1024]{1,0:T(8,128)S(1)} %copy-done, f32[16,1024]{1,0:T(8,128)S(1)} %copy-done.3, f32[32,8,1024]{2,1,0:T(8,128)S(1)} %get-tuple-element.16.gate, f32[32,8,1024]{2,1,0:T(8,128)S(1)} %get-tuple-element.17.local, ...), custom_call_target="tpu_custom_call" | custom-call | flops 1677721600 | bytes 8388608 | tf_op jit(solution)/shard_map/pallas_call | solution.py:224
  50.0 2.0 %collective-permute-done.9.refs_3_ = bf16[48,2048]{1,0:T(8,128)(2,1)S(1)} collective-permute-done((bf16[48,2048]{1,0:T(8,128)(2,1)S(1)}, bf16[48,2048]{1,0:T(8,128)(2,1)S(1)}, u32[]{:S(2)}, u32[]{:S(2)}) %collective-permute-start.9) | collective-permute-done | bytes 196640 | tf_op jit(solution)/shard_map/ppermute | solution.py:193
  52.6 2.6 %collective-permute-start.6 = (bf16[256,512]{1,0:T(8,128)(2,1)S(1)}, bf16[256,512]{1,0:T(8,128)(2,1)S(1)}, u32[]{:S(2)}, u32[]{:S(2)}) collective-permute-start(bf16[256,512]{1,0:T(8,128)(2,1)S(1)} %get-tuple-element.20), channel_id=1, source_target_pairs={{0,3},{1,11},{2,1},{3,9},{4,7},{5,15},{6,5},{7,13},{8,2},{9,10},{1... | collective-permute-start | bytes 786440 | tf_op jit(solution)/shard_map/ppermute | solution.py:396
  55.2 2.6 %collective-permute-start.20 = (bf16[128,1024]{1,0:T(8,128)(2,1)S(1)}, bf16[128,1024]{1,0:T(8,128)(2,1)S(1)}, u32[]{:S(2)}, u32[]{:S(2)}) collective-permute-start(bf16[128,1024]{1,0:T(8,128)(2,1)S(1)} %get-tuple-element.36), channel_id=1, source_target_pairs={{0,16},{4,20},{8,24},{12,28},{16,0},{20,4},{24,8},{28,12},{1,17},{... | collective-permute-start | bytes 786440 | tf_op jit(solution)/shard_map/ppermute | solution.py:193
  57.8 2.0 %collective-permute-start.11 = (bf16[128,2048]{1,0:T(8,128)(2,1)S(1)}, bf16[128,2048]{1,0:T(8,128)(2,1)S(1)}, u32[]{:S(2)}, u32[]{:S(2)}) collective-permute-start(bf16[128,2048]{1,0:T(8,128)(2,1)S(1)} %collective-permute-done.8.refs_2_), channel_id=1, source_target_pairs={{0,4},{4,0},{8,12},{12,8},{16,20},{20,16},{24,28},{28,24},{1,5},{5... | collective-permute-start | bytes 1572872 | tf_op jit(solution)/shard_map/ppermute | solution.py:193
  60.2 6.9 %collective-permute-done.6.from_1 = bf16[256,512]{1,0:T(8,128)(2,1)S(1)} collective-permute-done((bf16[256,512]{1,0:T(8,128)(2,1)S(1)}, bf16[256,512]{1,0:T(8,128)(2,1)S(1)}, u32[]{:S(2)}, u32[]{:S(2)}) %collective-permute-start.6) | collective-permute-done | bytes 262176 | tf_op jit(solution)/shard_map/ppermute | solution.py:396
  68.5 7.5 %collective-permute-done.20.refs_8_ = bf16[128,1024]{1,0:T(8,128)(2,1)S(1)} collective-permute-done((bf16[128,1024]{1,0:T(8,128)(2,1)S(1)}, bf16[128,1024]{1,0:T(8,128)(2,1)S(1)}, u32[]{:S(2)}, u32[]{:S(2)}) %collective-permute-start.20) | collective-permute-done | bytes 262176 | tf_op jit(solution)/shard_map/ppermute | solution.py:193
  76.0 1.8 %collective-permute-start.21 = (bf16[128,1024]{1,0:T(8,128)(2,1)S(1)}, bf16[128,1024]{1,0:T(8,128)(2,1)S(1)}, u32[]{:S(2)}, u32[]{:S(2)}) collective-permute-start(bf16[128,1024]{1,0:T(8,128)(2,1)S(1)} %collective-permute-done.20.refs_8_), channel_id=1, source_target_pairs={{0,4},{4,0},{8,12},{12,8},{16,20},{20,16},{24,28},{28,24},{1,5},{5... | collective-permute-start | bytes 786440 | tf_op jit(solution)/shard_map/ppermute | solution.py:193
  77.8 2.4 %collective-permute-done.14.refs_8_ = bf16[128,1024]{1,0:T(8,128)(2,1)S(1)} collective-permute-done((bf16[128,1024]{1,0:T(8,128)(2,1)S(1)}, bf16[128,1024]{1,0:T(8,128)(2,1)S(1)}, u32[]{:S(2)}, u32[]{:S(2)}) %collective-permute-start.14) | collective-permute-done | bytes 262176 | tf_op jit(solution)/shard_map/ppermute | solution.py:193
  80.2 1.9 %collective-permute-start.17 = (bf16[128,1024]{1,0:T(8,128)(2,1)S(1)}, bf16[128,1024]{1,0:T(8,128)(2,1)S(1)}, u32[]{:S(2)}, u32[]{:S(2)}) collective-permute-start(bf16[128,1024]{1,0:T(8,128)(2,1)S(1)} %collective-permute-done.14.refs_8_), channel_id=1, source_target_pairs={{0,4},{4,0},{8,12},{12,8},{16,20},{20,16},{24,28},{28,24},{1,5},{5... | collective-permute-start | bytes 786440 | tf_op jit(solution)/shard_map/ppermute | solution.py:193
  82.1 2.6 %collective-permute-done.21.refs_11_ = bf16[128,1024]{1,0:T(8,128)(2,1)S(1)} collective-permute-done((bf16[128,1024]{1,0:T(8,128)(2,1)S(1)}, bf16[128,1024]{1,0:T(8,128)(2,1)S(1)}, u32[]{:S(2)}, u32[]{:S(2)}) %collective-permute-start.21) | collective-permute-done | bytes 262176 | tf_op jit(solution)/shard_map/ppermute | solution.py:193
  84.7 2.7 %shard_map.68 = (bf16[512,512]{1,0:T(8,128)(2,1)S(1)}, f32[512,512]{1,0:T(8,128)S(1)}) custom-call(s32[6]{0:T(128)S(1)} %stack.31.flags, bf16[256,512]{1,0:T(8,128)(2,1)S(1)} %get-tuple-element.19.kept, bf16[256,512]{1,0:T(8,128)(2,1)S(1)} %collective-permute-done.4.from_q, bf16[256,512]{1,0:T(8,128)(2,1)S(1)} %collective-permute-done.5.from_r, ...), custom_call_target="tpu_custom_call" | custom-call | flops 1073741824 | bytes 5368709 | tf_op jit(solution)/shard_map/pallas_call | solution.py:224
  88.9 2.7 %shard_map.67 = (bf16[512,512]{1,0:T(8,128)(2,1)S(1)}, f32[512,512]{1,0:T(8,128)S(1)}) custom-call(s32[6]{0:T(128)S(1)} %stack.31.flags, bf16[256,512]{1,0:T(8,128)(2,1)S(1)} %get-tuple-element.19.kept, bf16[256,512]{1,0:T(8,128)(2,1)S(1)} %collective-permute-done.4.from_q, bf16[256,512]{1,0:T(8,128)(2,1)S(1)} %collective-permute-done.5.from_r, ...), custom_call_target="tpu_custom_call" | custom-call | flops 1073741824 | bytes 5368709 | tf_op jit(solution)/shard_map/pallas_call | solution.py:224
  94.2 6.9 %collective-permute-done.23 = bf16[256,512]{1,0:T(8,128)(2,1)S(1)} collective-permute-done((bf16[256,512]{1,0:T(8,128)(2,1)S(1)}, bf16[256,512]{1,0:T(8,128)(2,1)S(1)}, u32[]{:S(2)}, u32[]{:S(2)}) %collective-permute-start.23) | collective-permute-done | bytes 262176 | tf_op jit(solution)/shard_map/ppermute | solution.py:193
  101.1 5.1 %collective-permute-done.19 = bf16[256,512]{1,0:T(8,128)(2,1)S(1)} collective-permute-done((bf16[256,512]{1,0:T(8,128)(2,1)S(1)}, bf16[256,512]{1,0:T(8,128)(2,1)S(1)}, u32[]{:S(2)}, u32[]{:S(2)}) %collective-permute-start.19) | collective-permute-done | bytes 262176 | tf_op jit(solution)/shard_map/ppermute | solution.py:193
  (57 shorter events, 19.0 us)
Async XLA Ops:
  1.2 51.4 %collective-permute-start.13 = (bf16[80,2048]{1,0:T(8,128)(2,1)S(1)}, bf16[80,2048]{1,0:T(8,128)(2,1)S(1)}, u32[]{:S(2)}, u32[]{:S(2)}) collective-permute-start(bf16[80,2048]{1,0:T(8,128)(2,1)S(1)} %slice_select_fusion.refs_1_), channel_id=1, source_target_pairs={{0,16},{4,20},{8,24},{12,28},{16,0},{20,4},{24,8},{28,12},{1,17},{... | collective-permute-start | bytes 983048 | tf_op jit(solution)/shard_map/ppermute | solution.py:193
  5.4 49.9 %collective-permute-start.10 = (bf16[80,2048]{1,0:T(8,128)(2,1)S(1)}, bf16[80,2048]{1,0:T(8,128)(2,1)S(1)}, u32[]{:S(2)}, u32[]{:S(2)}) collective-permute-start(bf16[80,2048]{1,0:T(8,128)(2,1)S(1)} %slice_select_fusion.refs_1_), channel_id=1, source_target_pairs={{0,4},{4,0},{8,12},{12,8},{16,20},{20,16},{24,28},{28,24},{1,5},{5... | collective-permute-start | bytes 983048 | tf_op jit(solution)/shard_map/ppermute | solution.py:193
  7.7 6.1 %collective-permute-start = (bf16[2,3,1024]{2,0,1:T(2,128)(2,1)S(1)}, bf16[2,3,1024]{2,0,1:T(2,128)(2,1)S(1)}, u32[]{:S(2)}, u32[]{:S(2)}) collective-permute-start(bf16[2,3,1024]{2,0,1:T(2,128)(2,1)S(1)} %slice.80), channel_id=1, source_target_pairs={{0,4},{4,8},{8,12},{12,16},{16,20},{20,24},{24,28},{1,5},{5,9},{9,... | collective-permute-start | bytes 36872 | tf_op jit(solution)/shard_map/ppermute | solution.py:243
  16.9 4.7 %collective-permute-start.1 = (f32[16,1024]{1,0:T(8,128)S(1)}, f32[16,1024]{1,0:T(8,128)S(1)}, u32[]{:S(2)}, u32[]{:S(2)}) collective-permute-start(f32[16,1024]{1,0:T(8,128)S(1)} %get-tuple-element.18), channel_id=1, source_target_pairs={{0,8},{4,12},{8,0},{12,4},{16,24},{20,28},{24,16},{28,20},{1,9},{5... | collective-permute-start | bytes 196616 | tf_op jit(solution)/shard_map/ppermute | solution.py:193
  19.4 30.5 %collective-permute-start.8 = (bf16[128,2048]{1,0:T(8,128)(2,1)S(1)}, bf16[128,2048]{1,0:T(8,128)(2,1)S(1)}, u32[]{:S(2)}, u32[]{:S(2)}) collective-permute-start(bf16[128,2048]{1,0:T(8,128)(2,1)S(1)} %maximum_select_fusion), channel_id=1, source_target_pairs={{0,2},{1,3},{2,0},{3,1},{4,6},{5,7},{6,4},{7,5},{8,10},{9,11},{10,... | collective-permute-start | bytes 1572872 | tf_op jit(solution)/shard_map/ppermute | solution.py:193
  21.6 12.4 %collective-permute-start.2 = (f32[16,1024]{1,0:T(8,128)S(1)}, f32[16,1024]{1,0:T(8,128)S(1)}, u32[]{:S(2)}, u32[]{:S(2)}) collective-permute-start(f32[16,1024]{1,0:T(8,128)S(1)} %select_add_fusion.1), channel_id=1, source_target_pairs={{0,16},{4,20},{8,24},{12,28},{16,0},{20,4},{24,8},{28,12},{1,17},{... | collective-permute-start | bytes 196616 | tf_op jit(solution)/shard_map/ppermute | solution.py:193
  32.5 12.9 %collective-permute-start.12 = (bf16[48,2048]{1,0:T(8,128)(2,1)S(1)}, bf16[48,2048]{1,0:T(8,128)(2,1)S(1)}, u32[]{:S(2)}, u32[]{:S(2)}) collective-permute-start(bf16[48,2048]{1,0:T(8,128)(2,1)S(1)} %slice_select_fusion.1.refs_0_), channel_id=1, source_target_pairs={{0,16},{4,20},{8,24},{12,28},{16,0},{20,4},{24,8},{28,12},{1,17},{... | collective-permute-start | bytes 589832 | tf_op jit(solution)/shard_map/ppermute | solution.py:193
  34.0 11.5 %collective-permute-start.3 = (f32[16,1024]{1,0:T(8,128)S(1)}, f32[16,1024]{1,0:T(8,128)S(1)}, u32[]{:S(2)}, u32[]{:S(2)}) collective-permute-start(f32[16,1024]{1,0:T(8,128)S(1)} %add_select_fusion), channel_id=1, source_target_pairs={{0,4},{4,0},{8,12},{12,8},{16,20},{20,16},{24,28},{28,24},{1,5},{5... | collective-permute-start | bytes 196616 | tf_op jit(solution)/shard_map/ppermute | solution.py:193
  45.5 6.5 %collective-permute-start.9 = (bf16[48,2048]{1,0:T(8,128)(2,1)S(1)}, bf16[48,2048]{1,0:T(8,128)(2,1)S(1)}, u32[]{:S(2)}, u32[]{:S(2)}) collective-permute-start(bf16[48,2048]{1,0:T(8,128)(2,1)S(1)} %slice_select_fusion.1.refs_0_), channel_id=1, source_target_pairs={{0,4},{4,0},{8,12},{12,8},{16,20},{20,16},{24,28},{28,24},{1,5},{5... | collective-permute-start | bytes 589832 | tf_op jit(solution)/shard_map/ppermute | solution.py:193
  45.6 12.3 %collective-permute-start.15 = (bf16[48,2048]{1,0:T(8,128)(2,1)S(1)}, bf16[48,2048]{1,0:T(8,128)(2,1)S(1)}, u32[]{:S(2)}, u32[]{:S(2)}) collective-permute-start(bf16[48,2048]{1,0:T(8,128)(2,1)S(1)} %collective-permute-done.12.refs_6_), channel_id=1, source_target_pairs={{0,4},{4,0},{8,12},{12,8},{16,20},{20,16},{24,28},{28,24},{1,5},{5... | collective-permute-start | bytes 589832 | tf_op jit(solution)/shard_map/ppermute | solution.py:193
  49.9 10.0 %collective-permute-start.4 = (bf16[256,512]{1,0:T(8,128)(2,1)S(1)}, bf16[256,512]{1,0:T(8,128)(2,1)S(1)}, u32[]{:S(2)}, u32[]{:S(2)}) collective-permute-start(bf16[256,512]{1,0:T(8,128)(2,1)S(1)} %get-tuple-element.20), channel_id=1, source_target_pairs={{0,1},{1,9},{2,3},{3,11},{4,5},{5,13},{6,7},{7,15},{8,0},{9,8},{10... | collective-permute-start | bytes 786440 | tf_op jit(solution)/shard_map/ppermute | solution.py:396
  52.0 7.9 %collective-permute-start.5 = (bf16[256,512]{1,0:T(8,128)(2,1)S(1)}, bf16[256,512]{1,0:T(8,128)(2,1)S(1)}, u32[]{:S(2)}, u32[]{:S(2)}) collective-permute-start(bf16[256,512]{1,0:T(8,128)(2,1)S(1)} %get-tuple-element.19.kept), channel_id=1, source_target_pairs={{1,8},{3,10},{5,12},{7,14},{8,1},{10,3},{12,5},{14,7},{17,24},{19,... | collective-permute-start | bytes 786440 | tf_op jit(solution)/shard_map/ppermute | solution.py:396
  52.6 14.5 %collective-permute-start.6 = (bf16[256,512]{1,0:T(8,128)(2,1)S(1)}, bf16[256,512]{1,0:T(8,128)(2,1)S(1)}, u32[]{:S(2)}, u32[]{:S(2)}) collective-permute-start(bf16[256,512]{1,0:T(8,128)(2,1)S(1)} %get-tuple-element.20), channel_id=1, source_target_pairs={{0,3},{1,11},{2,1},{3,9},{4,7},{5,15},{6,5},{7,13},{8,2},{9,10},{1... | collective-permute-start | bytes 786440 | tf_op jit(solution)/shard_map/ppermute | solution.py:396
  55.2 20.8 %collective-permute-start.20 = (bf16[128,1024]{1,0:T(8,128)(2,1)S(1)}, bf16[128,1024]{1,0:T(8,128)(2,1)S(1)}, u32[]{:S(2)}, u32[]{:S(2)}) collective-permute-start(bf16[128,1024]{1,0:T(8,128)(2,1)S(1)} %get-tuple-element.36), channel_id=1, source_target_pairs={{0,16},{4,20},{8,24},{12,28},{16,0},{20,4},{24,8},{28,12},{1,17},{... | collective-permute-start | bytes 786440 | tf_op jit(solution)/shard_map/ppermute | solution.py:193
  57.8 26.9 %collective-permute-start.11 = (bf16[128,2048]{1,0:T(8,128)(2,1)S(1)}, bf16[128,2048]{1,0:T(8,128)(2,1)S(1)}, u32[]{:S(2)}, u32[]{:S(2)}) collective-permute-start(bf16[128,2048]{1,0:T(8,128)(2,1)S(1)} %collective-permute-done.8.refs_2_), channel_id=1, source_target_pairs={{0,4},{4,0},{8,12},{12,8},{16,20},{20,16},{24,28},{28,24},{1,5},{5... | collective-permute-start | bytes 1572872 | tf_op jit(solution)/shard_map/ppermute | solution.py:193
  59.8 22.3 %collective-permute-start.16 = (bf16[80,2048]{1,0:T(8,128)(2,1)S(1)}, bf16[80,2048]{1,0:T(8,128)(2,1)S(1)}, u32[]{:S(2)}, u32[]{:S(2)}) collective-permute-start(bf16[80,2048]{1,0:T(8,128)(2,1)S(1)} %collective-permute-done.13.refs_7_), channel_id=1, source_target_pairs={{0,4},{4,0},{8,12},{12,8},{16,20},{20,16},{24,28},{28,24},{1,5},{5... | collective-permute-start | bytes 983048 | tf_op jit(solution)/shard_map/ppermute | solution.py:193
  59.9 20.3 %collective-permute-start.14 = (bf16[128,1024]{1,0:T(8,128)(2,1)S(1)}, bf16[128,1024]{1,0:T(8,128)(2,1)S(1)}, u32[]{:S(2)}, u32[]{:S(2)}) collective-permute-start(bf16[128,1024]{1,0:T(8,128)(2,1)S(1)} %get-tuple-element.35), channel_id=1, source_target_pairs={{0,16},{4,20},{8,24},{12,28},{16,0},{20,4},{24,8},{28,12},{1,17},{... | collective-permute-start | bytes 786440 | tf_op jit(solution)/shard_map/ppermute | solution.py:193
  67.1 15.0 %collective-permute-start.7 = (bf16[256,512]{1,0:T(8,128)(2,1)S(1)}, bf16[256,512]{1,0:T(8,128)(2,1)S(1)}, u32[]{:S(2)}, u32[]{:S(2)}) collective-permute-start(bf16[256,512]{1,0:T(8,128)(2,1)S(1)} %get-tuple-element.19.kept), channel_id=1, source_target_pairs={{0,2},{1,10},{2,0},{3,8},{4,6},{5,14},{6,4},{7,12},{8,3},{9,11},{1... | collective-permute-start | bytes 786440 | tf_op jit(solution)/shard_map/ppermute | solution.py:396
  76.0 8.7 %collective-permute-start.21 = (bf16[128,1024]{1,0:T(8,128)(2,1)S(1)}, bf16[128,1024]{1,0:T(8,128)(2,1)S(1)}, u32[]{:S(2)}, u32[]{:S(2)}) collective-permute-start(bf16[128,1024]{1,0:T(8,128)(2,1)S(1)} %collective-permute-done.20.refs_8_), channel_id=1, source_target_pairs={{0,4},{4,0},{8,12},{12,8},{16,20},{20,16},{24,28},{28,24},{1,5},{5... | collective-permute-start | bytes 786440 | tf_op jit(solution)/shard_map/ppermute | solution.py:193
  80.2 8.7 %collective-permute-start.17 = (bf16[128,1024]{1,0:T(8,128)(2,1)S(1)}, bf16[128,1024]{1,0:T(8,128)(2,1)S(1)}, u32[]{:S(2)}, u32[]{:S(2)}) collective-permute-start(bf16[128,1024]{1,0:T(8,128)(2,1)S(1)} %collective-permute-done.14.refs_8_), channel_id=1, source_target_pairs={{0,4},{4,0},{8,12},{12,8},{16,20},{20,16},{24,28},{28,24},{1,5},{5... | collective-permute-start | bytes 786440 | tf_op jit(solution)/shard_map/ppermute | solution.py:193
  87.4 4.2 %collective-permute-start.22 = (bf16[512,512]{1,0:T(8,128)(2,1)S(1)}, bf16[512,512]{1,0:T(8,128)(2,1)S(1)}, u32[]{:S(2)}, u32[]{:S(2)}) collective-permute-start(bf16[512,512]{1,0:T(8,128)(2,1)S(1)} %get-tuple-element.24), channel_id=1, source_target_pairs={{0,1},{1,0},{2,3},{3,2},{4,5},{5,4},{6,7},{7,6},{8,9},{9,8},{10,11... | collective-permute-start | bytes 1572872 | tf_op jit(solution)/shard_map/ppermute | solution.py:193
  91.5 2.0 %collective-permute-start.18 = (bf16[512,512]{1,0:T(8,128)(2,1)S(1)}, bf16[512,512]{1,0:T(8,128)(2,1)S(1)}, u32[]{:S(2)}, u32[]{:S(2)}) collective-permute-start(bf16[512,512]{1,0:T(8,128)(2,1)S(1)} %get-tuple-element.22), channel_id=1, source_target_pairs={{0,1},{1,0},{2,3},{3,2},{4,5},{5,4},{6,7},{7,6},{8,9},{9,8},{10,11... | collective-permute-start | bytes 1572872 | tf_op jit(solution)/shard_map/ppermute | solution.py:193
  91.8 9.2 %collective-permute-start.23 = (bf16[256,512]{1,0:T(8,128)(2,1)S(1)}, bf16[256,512]{1,0:T(8,128)(2,1)S(1)}, u32[]{:S(2)}, u32[]{:S(2)}) collective-permute-start(bf16[256,512]{1,0:T(8,128)(2,1)S(1)} %slice.124), channel_id=1, source_target_pairs={{0,8},{4,12},{8,0},{12,4},{16,24},{20,28},{24,16},{28,20},{1,9},{5... | collective-permute-start | bytes 786440 | tf_op jit(solution)/shard_map/ppermute | solution.py:193
  93.7 12.5 %collective-permute-start.19 = (bf16[256,512]{1,0:T(8,128)(2,1)S(1)}, bf16[256,512]{1,0:T(8,128)(2,1)S(1)}, u32[]{:S(2)}, u32[]{:S(2)}) collective-permute-start(bf16[256,512]{1,0:T(8,128)(2,1)S(1)} %slice.125), channel_id=1, source_target_pairs={{0,8},{4,12},{8,0},{12,4},{16,24},{20,28},{24,16},{28,20},{1,9},{5... | collective-permute-start | bytes 786440 | tf_op jit(solution)/shard_map/ppermute | solution.py:193
  (6 other events, 77.8 us)

commit v3 on v2

--- a/solution.py
+++ b/solution.py
@@ -10,7 +10,7 @@
 
 LANES = 128
 CHUNKS = 2
-UNROLL = 16
+UNROLL = 32
 CUTS = (3,)
 CORE_FIRST, PART_FIRST, ONE_PART = range(3)
 SEGS = 8
@@ -297,15 +297,15 @@
                     ]
 
 
-def cube_kernel(piece, orders, part, flags, kept, from_q, from_r, from_1, from_2, *refs):
+def cube_kernel(piece, orders, part, flags, kept, from_q, from_r, from_1, from_2, across, *refs):
     weights, (theirs, mine, left) = refs[:-3], refs[-3:]
     width = mine.shape[1]
     full = weights[0].shape[1] // 2
-    tile = min(width, 256)
+    tile = min(width, 512)
 
     for stays, own, other in (
-        (1, (kept, from_q), (from_2, from_1)),
-        (0, (from_q, from_r), (from_1, from_2)),
+        (1, (kept, from_q), (from_2, across)),
+        (0, (from_q, from_r), (from_1, across)),
     ):
         for same, near_plane, far_plane in ((1, own, other), (0, other, own)):
 
@@ -329,7 +329,7 @@
             out[:, pl.ds(pl.multiple_of(i * tile, tile), tile)] = total.astype(out.dtype)
             return 0
 
-        lax.fori_loop(0, width // tile, one_tile, 0)
+        lax.fori_loop(0, width // tile, one_tile, 0, unroll=True)
 
 
 def cube_product(flags, gated, weights, piece, width, part):
@@ -354,7 +354,7 @@
 
 def project_cube(leaves, turns, flags, residual, out_weight, chunks):
     ctx, tp = lax.axis_size("ctx"), lax.axis_size("tp")
-    _, y, _, _, _ = cube_place()
+    core, y, _, zp, _ = cube_place()
     piece, columns = out_weight.shape
     channels = columns // tp
     width = channels // chunks
@@ -389,22 +389,17 @@
             else:
                 moves["gate_q"].append((source, over + ti))
                 moves["gate_r"].append((source, over + (ti ^ 1)))
-                moves["gate_1"].append((source, over + (ti ^ 2)))
-                moves["gate_2"].append((source, over + (ti ^ 3)))
 
     def move(value, name):
         return lax.ppermute(value, ("ctx", "tp"), moves[name])
 
-    gated = (
-        turns,
-        move(leaves, "gate_q"),
-        move(turns, "gate_r"),
-        move(leaves, "gate_1"),
-        move(turns, "gate_2"),
-    )
+    from_q, from_r = move(leaves, "gate_q"), move(turns, "gate_r")
+    from_1, from_2 = move(leaves, "gate_1"), move(turns, "gate_2")
+    across = flip(jnp.where(core == zp, from_q, from_r), "tp", 2)
+    gated = (turns, from_q, from_r, from_1, from_2, across)
 
     rows = residual.shape[0]
-    outs = []
+    out = residual
     for j in range(chunks):
         weights = [(w, CORE_FIRST) for w in near] + [(take, PART_FIRST)]
         weights += [(w, CORE_FIRST) for w in near_x] + [(take_x, PART_FIRST)]
@@ -414,8 +409,9 @@
         total = ours + flip(theirs, "tp", 1).astype(jnp.float32)
         pair = flip(total[rows:].astype(jnp.bfloat16), "ctx", 2)
         base = residual[:, j * width : (j + 1) * width].astype(jnp.float32)
-        outs.append((base + (total[:rows] + pair.astype(jnp.float32))).astype(jnp.bfloat16))
-    return jnp.concatenate(outs, axis=1)
+        value = (base + (total[:rows] + pair.astype(jnp.float32))).astype(jnp.bfloat16)
+        out = lax.dynamic_update_slice(out, value, (0, j * width))
+    return out
 
 
 def on_device(features, short_filter, log_decay, residue, residual, out_weight):

time: 108 us -> 110 us (1.019)
  waiting for transfers between devices: 39.8 us -> 43.3 us
  Pallas kernels: 15.6 us -> 13.8 us
    ppermute x19 -> x20, waiting for transfers between devices: 30.6 us -> 41 us  [flip(): return lax.ppermute(value, axis, [(i, i ^ bit) for i in range(count)])]
    ppermute x4, waiting for transfers between devices: 6.91 us -> 0.01 us  [move(): return lax.ppermute(value, ('ctx', 'tp'), moves[name])]
    pallas_call x5, Pallas kernels: 15.6 us -> 13.8 us  [in_vmem(): pl.pallas_call(kernel, out_shape=out_shape, in_specs=specs, out_specs=pl....]
    ppermute x19 -> x20, starting transfers between devices: 36.8 us -> 36.4 us  [flip(): return lax.ppermute(value, axis, [(i, i ^ bit) for i in range(count)])]
  transfers between devices with their start and end apart: 24 -> 25, of which waited for: 12 -> 11; matrix products, arithmetic and copies ran while one was open for 4% -> 4% of each run, Pallas kernels for 15% -> 13%
where the time goes in v3:
time: 110 us; the launch traced here: 109 us
  starting transfers between devices  44.3 us (40%)
  waiting for transfers between devices  43.3 us (39%)
  Pallas kernels  13.8 us (13%)
  local copies, waits for them, and re-layouts  3.84 us (3%)
  other arithmetic  3.79 us (3%)
    ppermute x20, waiting for transfers between devices, flip(): return lax.ppermute(value, axis, [(i, i ^ bit) for i in range(count)])  41 us
    ppermute x20, starting transfers between devices, flip(): return lax.ppermute(value, axis, [(i, i ^ bit) for i in range(count)])  36.4 us
    pallas_call x5, Pallas kernels, in_vmem(): pl.pallas_call(kernel, out_shape=out_shape, in_specs=specs, out_specs=pl....  13.8 us
    ppermute x4, starting transfers between devices, move(): return lax.ppermute(value, ('ctx', 'tp'), moves[name])  5.47 us
    ppermute x1, starting transfers between devices, gated_blocks(): lax.ppermute(features[tok_rows - (filter_len - 1):], 'ctx', [(i, i + 1) f...  2.44 us
    ppermute x1, waiting for transfers between devices, gated_blocks(): lax.ppermute(features[tok_rows - (filter_len - 1):], 'ctx', [(i, i + 1) f...  2.28 us
    select_n x2, other arithmetic, project_cube(): jnp.where(y == 0, sides[0][lo:hi], sides[1][lo:hi])  2.27 us
  transfers between devices with their start and end apart: 25, of which 11 were waited for; matrix products, arithmetic and copies ran while one was open for 4% of the time, Pallas kernels for 13%

profile of v3, /device:TPU:0, one launch (start us, length us, event | category | flops | bytes accessed | tf_op | source)
XLA Modules:
  0.0 109.4 jit_solution(5946451860910074876)
XLA Ops:
  1.2 4.1 %collective-permute-start.14 = (bf16[80,2048]{1,0:T(8,128)(2,1)S(1)}, bf16[80,2048]{1,0:T(8,128)(2,1)S(1)}, u32[]{:S(2)}, u32[]{:S(2)}) collective-permute-start(bf16[80,2048]{1,0:T(8,128)(2,1)S(1)} %slice_select_fusion.refs_1_), channel_id=1, source_target_pairs={{0,16},{4,20},{8,24},{12,28},{16,0},{20,4},{24,8},{28,12},{1,17},{... | collective-permute-start | bytes 983048 | tf_op jit(solution)/shard_map/ppermute | solution.py:193
  5.4 1.5 %collective-permute-start.11 = (bf16[80,2048]{1,0:T(8,128)(2,1)S(1)}, bf16[80,2048]{1,0:T(8,128)(2,1)S(1)}, u32[]{:S(2)}, u32[]{:S(2)}) collective-permute-start(bf16[80,2048]{1,0:T(8,128)(2,1)S(1)} %slice_select_fusion.refs_1_), channel_id=1, source_target_pairs={{0,4},{4,0},{8,12},{12,8},{16,20},{20,16},{24,28},{28,24},{1,5},{5... | collective-permute-start | bytes 983048 | tf_op jit(solution)/shard_map/ppermute | solution.py:193
  7.7 2.4 %collective-permute-start = (bf16[2,3,1024]{2,0,1:T(2,128)(2,1)S(1)}, bf16[2,3,1024]{2,0,1:T(2,128)(2,1)S(1)}, u32[]{:S(2)}, u32[]{:S(2)}) collective-permute-start(bf16[2,3,1024]{2,0,1:T(2,128)(2,1)S(1)} %slice.80), channel_id=1, source_target_pairs={{0,4},{4,8},{8,12},{12,16},{16,20},{20,24},{24,28},{1,5},{5,9},{9,... | collective-permute-start | bytes 36872 | tf_op jit(solution)/shard_map/ppermute | solution.py:243
  11.5 2.3 %collective-permute-done = bf16[2,3,1024]{2,0,1:T(2,128)(2,1)S(1)} collective-permute-done((bf16[2,3,1024]{2,0,1:T(2,128)(2,1)S(1)}, bf16[2,3,1024]{2,0,1:T(2,128)(2,1)S(1)}, u32[]{:S(2)}, u32[]{:S(2)}) %collective-permute-start) | collective-permute-done | bytes 12320 | tf_op jit(solution)/shard_map/ppermute | solution.py:243
  13.8 2.7 %shard_map.64 = (f32[16,1024]{1,0:T(8,128)S(1)}, f32[16,8,1024]{2,1,0:T(8,128)S(1)}) custom-call(bf16[3,256,1024]{2,1,0:T(8,128)(2,1)S(1)} %bitcast.8, bf16[3,2,1024]{2,1,0:T(2,128)(2,1)S(1)} %bitcast.10, f32[3,3,1024]{2,1,0:T(4,128)S(1)} %copy-done.4, f32[16,1024]{1,0:T(8,128)S(1)} %copy-done), custom_call_target="tpu_custom_call" | custom-call | flops 1677721600 | bytes 8388608 | tf_op jit(solution)/shard_map/pallas_call | solution.py:224
  16.6 2.4 %collective-permute-start.1 = (f32[16,1024]{1,0:T(8,128)S(1)}, f32[16,1024]{1,0:T(8,128)S(1)}, u32[]{:S(2)}, u32[]{:S(2)}) collective-permute-start(f32[16,1024]{1,0:T(8,128)S(1)} %get-tuple-element.18), channel_id=1, source_target_pairs={{0,8},{4,12},{8,0},{12,4},{16,24},{20,28},{24,16},{28,20},{1,9},{5... | collective-permute-start | bytes 196616 | tf_op jit(solution)/shard_map/ppermute | solution.py:193
  19.1 1.6 %collective-permute-start.9 = (bf16[128,2048]{1,0:T(8,128)(2,1)S(1)}, bf16[128,2048]{1,0:T(8,128)(2,1)S(1)}, u32[]{:S(2)}, u32[]{:S(2)}) collective-permute-start(bf16[128,2048]{1,0:T(8,128)(2,1)S(1)} %maximum_select_fusion), channel_id=1, source_target_pairs={{0,2},{1,3},{2,0},{3,1},{4,6},{5,7},{6,4},{7,5},{8,10},{9,11},{10,... | collective-permute-start | bytes 1572872 | tf_op jit(solution)/shard_map/ppermute | solution.py:193
  21.5 9.6 %collective-permute-start.2 = (f32[16,1024]{1,0:T(8,128)S(1)}, f32[16,1024]{1,0:T(8,128)S(1)}, u32[]{:S(2)}, u32[]{:S(2)}) collective-permute-start(f32[16,1024]{1,0:T(8,128)S(1)} %select_add_fusion.1), channel_id=1, source_target_pairs={{0,16},{4,20},{8,24},{12,28},{16,0},{20,4},{24,8},{28,12},{1,17},{... | collective-permute-start | bytes 196616 | tf_op jit(solution)/shard_map/ppermute | solution.py:193
  33.7 5.0 %collective-permute-start.3 = (f32[16,1024]{1,0:T(8,128)S(1)}, f32[16,1024]{1,0:T(8,128)S(1)}, u32[]{:S(2)}, u32[]{:S(2)}) collective-permute-start(f32[16,1024]{1,0:T(8,128)S(1)} %add_select_fusion), channel_id=1, source_target_pairs={{0,4},{4,0},{8,12},{12,8},{16,20},{20,16},{24,28},{28,24},{1,5},{5... | collective-permute-start | bytes 196616 | tf_op jit(solution)/shard_map/ppermute | solution.py:193
  38.8 1.4 %copy-done.2 = bf16[256,3,1024]{2,0,1:T(8,128)(2,1)S(1)} copy-done((bf16[256,3,1024]{2,0,1:T(8,128)(2,1)S(1)}, bf16[256,3,1024]{2,0,1:T(8,128)(2,1)}, u32[]{:S(2)}) %copy-start.2) | copy-done | bytes 1572888
  40.2 4.7 %shard_map.65 = (f32[32,8,1024]{2,1,0:T(8,128)S(1)}, f32[32,8,1024]{2,1,0:T(8,128)S(1)}) custom-call(bf16[3,256,1024]{2,1,0:T(8,128)(2,1)S(1)} %bitcast.9, bf16[3,2,1024]{2,1,0:T(2,128)(2,1)S(1)} %bitcast.11, f32[3,3,1024]{2,1,0:T(4,128)S(1)} %copy-done.4, f32[16,1024]{1,0:T(8,128)S(1)} %copy-done, f32[16,1024]{1,0:T(8,128)S(1)} %copy-done.3, ...), custom_call_target="tpu_custom_call" | custom-call | flops 1677721600 | bytes 8388608 | tf_op jit(solution)/shard_map/pallas_call | solution.py:224
  45.0 2.2 %shard_map.66 = (bf16[256,512]{1,0:T(8,128)(2,1)S(1)}, bf16[256,512]{1,0:T(8,128)(2,1)S(1)}) custom-call(s32[6]{0:T(128)S(1)} %stack.31.flags, f32[16,1024]{1,0:T(8,128)S(1)} %copy-done, f32[16,1024]{1,0:T(8,128)S(1)} %copy-done.3, f32[32,8,1024]{2,1,0:T(8,128)S(1)} %get-tuple-element.16.gate, f32[32,8,1024]{2,1,0:T(8,128)S(1)} %get-tuple-element.17.local, ...), custom_call_target="tpu_custom_call" | custom-call | flops 1677721600 | bytes 8388608 | tf_op jit(solution)/shard_map/pallas_call | solution.py:224
  47.3 3.6 %collective-permute-done.10.refs_3_ = bf16[48,2048]{1,0:T(8,128)(2,1)S(1)} collective-permute-done((bf16[48,2048]{1,0:T(8,128)(2,1)S(1)}, bf16[48,2048]{1,0:T(8,128)(2,1)S(1)}, u32[]{:S(2)}, u32[]{:S(2)}) %collective-permute-start.10) | collective-permute-done | bytes 196640 | tf_op jit(solution)/shard_map/ppermute | solution.py:193
  50.8 1.7 %collective-permute-start.16 = (bf16[48,2048]{1,0:T(8,128)(2,1)S(1)}, bf16[48,2048]{1,0:T(8,128)(2,1)S(1)}, u32[]{:S(2)}, u32[]{:S(2)}) collective-permute-start(bf16[48,2048]{1,0:T(8,128)(2,1)S(1)} %collective-permute-done.13.refs_6_), channel_id=1, source_target_pairs={{0,4},{4,0},{8,12},{12,8},{16,20},{20,16},{24,28},{28,24},{1,5},{5... | collective-permute-start | bytes 589832 | tf_op jit(solution)/shard_map/ppermute | solution.py:193
  54.6 3.4 %collective-permute-start.7 = (bf16[256,512]{1,0:T(8,128)(2,1)S(1)}, bf16[256,512]{1,0:T(8,128)(2,1)S(1)}, u32[]{:S(2)}, u32[]{:S(2)}) collective-permute-start(bf16[256,512]{1,0:T(8,128)(2,1)S(1)} %get-tuple-element.19.kept), channel_id=1, source_target_pairs={{0,2},{2,0},{4,6},{6,4},{9,11},{11,9},{13,15},{15,13},{16,18},{18,... | collective-permute-start | bytes 786440 | tf_op jit(solution)/shard_map/ppermute | solution.py:394
  60.4 2.7 %collective-permute-start.21 = (bf16[128,1024]{1,0:T(8,128)(2,1)S(1)}, bf16[128,1024]{1,0:T(8,128)(2,1)S(1)}, u32[]{:S(2)}, u32[]{:S(2)}) collective-permute-start(bf16[128,1024]{1,0:T(8,128)(2,1)S(1)} %get-tuple-element.33), channel_id=1, source_target_pairs={{0,16},{4,20},{8,24},{12,28},{16,0},{20,4},{24,8},{28,12},{1,17},{... | collective-permute-start | bytes 786440 | tf_op jit(solution)/shard_map/ppermute | solution.py:193
  64.4 15.3 %collective-permute-done.15.refs_8_ = bf16[128,1024]{1,0:T(8,128)(2,1)S(1)} collective-permute-done((bf16[128,1024]{1,0:T(8,128)(2,1)S(1)}, bf16[128,1024]{1,0:T(8,128)(2,1)S(1)}, u32[]{:S(2)}, u32[]{:S(2)}) %collective-permute-start.15) | collective-permute-done | bytes 262176 | tf_op jit(solution)/shard_map/ppermute | solution.py:193
  80.0 3.6 %collective-permute-done.21.refs_8_ = bf16[128,1024]{1,0:T(8,128)(2,1)S(1)} collective-permute-done((bf16[128,1024]{1,0:T(8,128)(2,1)S(1)}, bf16[128,1024]{1,0:T(8,128)(2,1)S(1)}, u32[]{:S(2)}, u32[]{:S(2)}) %collective-permute-start.21) | collective-permute-done | bytes 262176 | tf_op jit(solution)/shard_map/ppermute | solution.py:193
  83.6 1.7 %collective-permute-start.22 = (bf16[128,1024]{1,0:T(8,128)(2,1)S(1)}, bf16[128,1024]{1,0:T(8,128)(2,1)S(1)}, u32[]{:S(2)}, u32[]{:S(2)}) collective-permute-start(bf16[128,1024]{1,0:T(8,128)(2,1)S(1)} %collective-permute-done.21.refs_8_), channel_id=1, source_target_pairs={{0,4},{4,0},{8,12},{12,8},{16,20},{20,16},{24,28},{28,24},{1,5},{5... | collective-permute-start | bytes 786440 | tf_op jit(solution)/shard_map/ppermute | solution.py:193
  86.5 2.1 %shard_map.67 = (bf16[512,512]{1,0:T(8,128)(2,1)S(1)}, f32[512,512]{1,0:T(8,128)S(1)}) custom-call(s32[6]{0:T(128)S(1)} %stack.31.flags, bf16[256,512]{1,0:T(8,128)(2,1)S(1)} %get-tuple-element.19.kept, bf16[256,512]{1,0:T(8,128)(2,1)S(1)} %collective-permute-done.4.from_q, bf16[256,512]{1,0:T(8,128)(2,1)S(1)} %collective-permute-done.5.from_r, ...), custom_call_target="tpu_custom_call" | custom-call | flops 1073741824 | bytes 5368709 | tf_op jit(solution)/shard_map/pallas_call | solution.py:224
  88.7 3.1 %collective-permute-done.22.refs_11_ = bf16[128,1024]{1,0:T(8,128)(2,1)S(1)} collective-permute-done((bf16[128,1024]{1,0:T(8,128)(2,1)S(1)}, bf16[128,1024]{1,0:T(8,128)(2,1)S(1)}, u32[]{:S(2)}, u32[]{:S(2)}) %collective-permute-start.22) | collective-permute-done | bytes 262176 | tf_op jit(solution)/shard_map/ppermute | solution.py:193
  91.7 2.1 %shard_map.68 = (bf16[512,512]{1,0:T(8,128)(2,1)S(1)}, f32[512,512]{1,0:T(8,128)S(1)}) custom-call(s32[6]{0:T(128)S(1)} %stack.31.flags, bf16[256,512]{1,0:T(8,128)(2,1)S(1)} %get-tuple-element.19.kept, bf16[256,512]{1,0:T(8,128)(2,1)S(1)} %collective-permute-done.4.from_q, bf16[256,512]{1,0:T(8,128)(2,1)S(1)} %collective-permute-done.5.from_r, ...), custom_call_target="tpu_custom_call" | custom-call | flops 1073741824 | bytes 5368709 | tf_op jit(solution)/shard_map/pallas_call | solution.py:224
  97.0 6.4 %collective-permute-done.20 = bf16[256,512]{1,0:T(8,128)(2,1)S(1)} collective-permute-done((bf16[256,512]{1,0:T(8,128)(2,1)S(1)}, bf16[256,512]{1,0:T(8,128)(2,1)S(1)}, u32[]{:S(2)}, u32[]{:S(2)}) %collective-permute-start.20) | collective-permute-done | bytes 262176 | tf_op jit(solution)/shard_map/ppermute | solution.py:193
  103.5 5.0 %collective-permute-done.24 = bf16[256,512]{1,0:T(8,128)(2,1)S(1)} collective-permute-done((bf16[256,512]{1,0:T(8,128)(2,1)S(1)}, bf16[256,512]{1,0:T(8,128)(2,1)S(1)}, u32[]{:S(2)}, u32[]{:S(2)}) %collective-permute-start.24) | collective-permute-done | bytes 262176 | tf_op jit(solution)/shard_map/ppermute | solution.py:193
  (64 shorter events, 18.4 us)
Async XLA Ops:
  1.2 51.3 %collective-permute-start.14 = (bf16[80,2048]{1,0:T(8,128)(2,1)S(1)}, bf16[80,2048]{1,0:T(8,128)(2,1)S(1)}, u32[]{:S(2)}, u32[]{:S(2)}) collective-permute-start(bf16[80,2048]{1,0:T(8,128)(2,1)S(1)} %slice_select_fusion.refs_1_), channel_id=1, source_target_pairs={{0,16},{4,20},{8,24},{12,28},{16,0},{20,4},{24,8},{28,12},{1,17},{... | collective-permute-start | bytes 983048 | tf_op jit(solution)/shard_map/ppermute | solution.py:193
  5.4 49.2 %collective-permute-start.11 = (bf16[80,2048]{1,0:T(8,128)(2,1)S(1)}, bf16[80,2048]{1,0:T(8,128)(2,1)S(1)}, u32[]{:S(2)}, u32[]{:S(2)}) collective-permute-start(bf16[80,2048]{1,0:T(8,128)(2,1)S(1)} %slice_select_fusion.refs_1_), channel_id=1, source_target_pairs={{0,4},{4,0},{8,12},{12,8},{16,20},{20,16},{24,28},{28,24},{1,5},{5... | collective-permute-start | bytes 983048 | tf_op jit(solution)/shard_map/ppermute | solution.py:193
  7.7 6.1 %collective-permute-start = (bf16[2,3,1024]{2,0,1:T(2,128)(2,1)S(1)}, bf16[2,3,1024]{2,0,1:T(2,128)(2,1)S(1)}, u32[]{:S(2)}, u32[]{:S(2)}) collective-permute-start(bf16[2,3,1024]{2,0,1:T(2,128)(2,1)S(1)} %slice.80), channel_id=1, source_target_pairs={{0,4},{4,8},{8,12},{12,16},{16,20},{20,24},{24,28},{1,5},{5,9},{9,... | collective-permute-start | bytes 36872 | tf_op jit(solution)/shard_map/ppermute | solution.py:243
  16.6 4.9 %collective-permute-start.1 = (f32[16,1024]{1,0:T(8,128)S(1)}, f32[16,1024]{1,0:T(8,128)S(1)}, u32[]{:S(2)}, u32[]{:S(2)}) collective-permute-start(f32[16,1024]{1,0:T(8,128)S(1)} %get-tuple-element.18), channel_id=1, source_target_pairs={{0,8},{4,12},{8,0},{12,4},{16,24},{20,28},{24,16},{28,20},{1,9},{5... | collective-permute-start | bytes 196616 | tf_op jit(solution)/shard_map/ppermute | solution.py:193
  19.1 34.8 %collective-permute-start.9 = (bf16[128,2048]{1,0:T(8,128)(2,1)S(1)}, bf16[128,2048]{1,0:T(8,128)(2,1)S(1)}, u32[]{:S(2)}, u32[]{:S(2)}) collective-permute-start(bf16[128,2048]{1,0:T(8,128)(2,1)S(1)} %maximum_select_fusion), channel_id=1, source_target_pairs={{0,2},{1,3},{2,0},{3,1},{4,6},{5,7},{6,4},{7,5},{8,10},{9,11},{10,... | collective-permute-start | bytes 1572872 | tf_op jit(solution)/shard_map/ppermute | solution.py:193
  21.5 12.2 %collective-permute-start.2 = (f32[16,1024]{1,0:T(8,128)S(1)}, f32[16,1024]{1,0:T(8,128)S(1)}, u32[]{:S(2)}, u32[]{:S(2)}) collective-permute-start(f32[16,1024]{1,0:T(8,128)S(1)} %select_add_fusion.1), channel_id=1, source_target_pairs={{0,16},{4,20},{8,24},{12,28},{16,0},{20,4},{24,8},{28,12},{1,17},{... | collective-permute-start | bytes 196616 | tf_op jit(solution)/shard_map/ppermute | solution.py:193
  32.2 15.0 %collective-permute-start.13 = (bf16[48,2048]{1,0:T(8,128)(2,1)S(1)}, bf16[48,2048]{1,0:T(8,128)(2,1)S(1)}, u32[]{:S(2)}, u32[]{:S(2)}) collective-permute-start(bf16[48,2048]{1,0:T(8,128)(2,1)S(1)} %slice_select_fusion.1.refs_0_), channel_id=1, source_target_pairs={{0,16},{4,20},{8,24},{12,28},{16,0},{20,4},{24,8},{28,12},{1,17},{... | collective-permute-start | bytes 589832 | tf_op jit(solution)/shard_map/ppermute | solution.py:193
  33.7 11.1 %collective-permute-start.3 = (f32[16,1024]{1,0:T(8,128)S(1)}, f32[16,1024]{1,0:T(8,128)S(1)}, u32[]{:S(2)}, u32[]{:S(2)}) collective-permute-start(f32[16,1024]{1,0:T(8,128)S(1)} %add_select_fusion), channel_id=1, source_target_pairs={{0,4},{4,0},{8,12},{12,8},{16,20},{20,16},{24,28},{28,24},{1,5},{5... | collective-permute-start | bytes 196616 | tf_op jit(solution)/shard_map/ppermute | solution.py:193
  44.9 6.0 %collective-permute-start.10 = (bf16[48,2048]{1,0:T(8,128)(2,1)S(1)}, bf16[48,2048]{1,0:T(8,128)(2,1)S(1)}, u32[]{:S(2)}, u32[]{:S(2)}) collective-permute-start(bf16[48,2048]{1,0:T(8,128)(2,1)S(1)} %slice_select_fusion.1.refs_0_), channel_id=1, source_target_pairs={{0,4},{4,0},{8,12},{12,8},{16,20},{20,16},{24,28},{28,24},{1,5},{5... | collective-permute-start | bytes 589832 | tf_op jit(solution)/shard_map/ppermute | solution.py:193
  47.2 11.2 %collective-permute-start.4 = (bf16[256,512]{1,0:T(8,128)(2,1)S(1)}, bf16[256,512]{1,0:T(8,128)(2,1)S(1)}, u32[]{:S(2)}, u32[]{:S(2)}) collective-permute-start(bf16[256,512]{1,0:T(8,128)(2,1)S(1)} %get-tuple-element.20), channel_id=1, source_target_pairs={{0,1},{1,9},{2,3},{3,11},{4,5},{5,13},{6,7},{7,15},{8,0},{9,8},{10... | collective-permute-start | bytes 786440 | tf_op jit(solution)/shard_map/ppermute | solution.py:394
  50.8 7.2 %collective-permute-start.16 = (bf16[48,2048]{1,0:T(8,128)(2,1)S(1)}, bf16[48,2048]{1,0:T(8,128)(2,1)S(1)}, u32[]{:S(2)}, u32[]{:S(2)}) collective-permute-start(bf16[48,2048]{1,0:T(8,128)(2,1)S(1)} %collective-permute-done.13.refs_6_), channel_id=1, source_target_pairs={{0,4},{4,0},{8,12},{12,8},{16,20},{20,16},{24,28},{28,24},{1,5},{5... | collective-permute-start | bytes 589832 | tf_op jit(solution)/shard_map/ppermute | solution.py:193
  52.6 7.8 %collective-permute-start.6 = (bf16[256,512]{1,0:T(8,128)(2,1)S(1)}, bf16[256,512]{1,0:T(8,128)(2,1)S(1)}, u32[]{:S(2)}, u32[]{:S(2)}) collective-permute-start(bf16[256,512]{1,0:T(8,128)(2,1)S(1)} %get-tuple-element.20), channel_id=1, source_target_pairs={{0,3},{2,1},{4,7},{6,5},{9,10},{11,8},{13,14},{15,12},{16,19},{18,... | collective-permute-start | bytes 786440 | tf_op jit(solution)/shard_map/ppermute | solution.py:394
  53.9 5.4 %collective-permute-start.5 = (bf16[256,512]{1,0:T(8,128)(2,1)S(1)}, bf16[256,512]{1,0:T(8,128)(2,1)S(1)}, u32[]{:S(2)}, u32[]{:S(2)}) collective-permute-start(bf16[256,512]{1,0:T(8,128)(2,1)S(1)} %get-tuple-element.19.kept), channel_id=1, source_target_pairs={{1,8},{3,10},{5,12},{7,14},{8,1},{10,3},{12,5},{14,7},{17,24},{19,... | collective-permute-start | bytes 786440 | tf_op jit(solution)/shard_map/ppermute | solution.py:394
  54.6 8.5 %collective-permute-start.7 = (bf16[256,512]{1,0:T(8,128)(2,1)S(1)}, bf16[256,512]{1,0:T(8,128)(2,1)S(1)}, u32[]{:S(2)}, u32[]{:S(2)}) collective-permute-start(bf16[256,512]{1,0:T(8,128)(2,1)S(1)} %get-tuple-element.19.kept), channel_id=1, source_target_pairs={{0,2},{2,0},{4,6},{6,4},{9,11},{11,9},{13,15},{15,13},{16,18},{18,... | collective-permute-start | bytes 786440 | tf_op jit(solution)/shard_map/ppermute | solution.py:394
  58.1 27.2 %collective-permute-start.12 = (bf16[128,2048]{1,0:T(8,128)(2,1)S(1)}, bf16[128,2048]{1,0:T(8,128)(2,1)S(1)}, u32[]{:S(2)}, u32[]{:S(2)}) collective-permute-start(bf16[128,2048]{1,0:T(8,128)(2,1)S(1)} %collective-permute-done.9.refs_2_), channel_id=1, source_target_pairs={{0,4},{4,0},{8,12},{12,8},{16,20},{20,16},{24,28},{28,24},{1,5},{5... | collective-permute-start | bytes 1572872 | tf_op jit(solution)/shard_map/ppermute | solution.py:193
  58.4 21.3 %collective-permute-start.15 = (bf16[128,1024]{1,0:T(8,128)(2,1)S(1)}, bf16[128,1024]{1,0:T(8,128)(2,1)S(1)}, u32[]{:S(2)}, u32[]{:S(2)}) collective-permute-start(bf16[128,1024]{1,0:T(8,128)(2,1)S(1)} %get-tuple-element.34), channel_id=1, source_target_pairs={{0,16},{4,20},{8,24},{12,28},{16,0},{20,4},{24,8},{28,12},{1,17},{... | collective-permute-start | bytes 786440 | tf_op jit(solution)/shard_map/ppermute | solution.py:193
  59.3 25.9 %collective-permute-start.17 = (bf16[80,2048]{1,0:T(8,128)(2,1)S(1)}, bf16[80,2048]{1,0:T(8,128)(2,1)S(1)}, u32[]{:S(2)}, u32[]{:S(2)}) collective-permute-start(bf16[80,2048]{1,0:T(8,128)(2,1)S(1)} %collective-permute-done.14.refs_7_), channel_id=1, source_target_pairs={{0,4},{4,0},{8,12},{12,8},{16,20},{20,16},{24,28},{28,24},{1,5},{5... | collective-permute-start | bytes 983048 | tf_op jit(solution)/shard_map/ppermute | solution.py:193
  60.4 23.2 %collective-permute-start.21 = (bf16[128,1024]{1,0:T(8,128)(2,1)S(1)}, bf16[128,1024]{1,0:T(8,128)(2,1)S(1)}, u32[]{:S(2)}, u32[]{:S(2)}) collective-permute-start(bf16[128,1024]{1,0:T(8,128)(2,1)S(1)} %get-tuple-element.33), channel_id=1, source_target_pairs={{0,16},{4,20},{8,24},{12,28},{16,0},{20,4},{24,8},{28,12},{1,17},{... | collective-permute-start | bytes 786440 | tf_op jit(solution)/shard_map/ppermute | solution.py:193
  63.1 22.1 %collective-permute-start.8 = (bf16[256,512]{1,0:T(8,128)(2,1)S(1)}, bf16[256,512]{1,0:T(8,128)(2,1)S(1)}, u32[]{:S(2)}, u32[]{:S(2)}) collective-permute-start(bf16[256,512]{1,0:T(8,128)(2,1)S(1)} %broadcast_select_fusion), channel_id=1, source_target_pairs={{0,2},{1,3},{2,0},{3,1},{4,6},{5,7},{6,4},{7,5},{8,10},{9,11},{10,... | collective-permute-start | bytes 786440 | tf_op jit(solution)/shard_map/ppermute | solution.py:193
  79.7 6.7 %collective-permute-start.18 = (bf16[128,1024]{1,0:T(8,128)(2,1)S(1)}, bf16[128,1024]{1,0:T(8,128)(2,1)S(1)}, u32[]{:S(2)}, u32[]{:S(2)}) collective-permute-start(bf16[128,1024]{1,0:T(8,128)(2,1)S(1)} %collective-permute-done.15.refs_8_), channel_id=1, source_target_pairs={{0,4},{4,0},{8,12},{12,8},{16,20},{20,16},{24,28},{28,24},{1,5},{5... | collective-permute-start | bytes 786440 | tf_op jit(solution)/shard_map/ppermute | solution.py:193
  83.6 8.2 %collective-permute-start.22 = (bf16[128,1024]{1,0:T(8,128)(2,1)S(1)}, bf16[128,1024]{1,0:T(8,128)(2,1)S(1)}, u32[]{:S(2)}, u32[]{:S(2)}) collective-permute-start(bf16[128,1024]{1,0:T(8,128)(2,1)S(1)} %collective-permute-done.21.refs_8_), channel_id=1, source_target_pairs={{0,4},{4,0},{8,12},{12,8},{16,20},{20,16},{24,28},{28,24},{1,5},{5... | collective-permute-start | bytes 786440 | tf_op jit(solution)/shard_map/ppermute | solution.py:193
  88.6 5.4 %collective-permute-start.19 = (bf16[512,512]{1,0:T(8,128)(2,1)S(1)}, bf16[512,512]{1,0:T(8,128)(2,1)S(1)}, u32[]{:S(2)}, u32[]{:S(2)}) collective-permute-start(bf16[512,512]{1,0:T(8,128)(2,1)S(1)} %get-tuple-element.22), channel_id=1, source_target_pairs={{0,1},{1,0},{2,3},{3,2},{4,5},{5,4},{6,7},{7,6},{8,9},{9,8},{10,11... | collective-permute-start | bytes 1572872 | tf_op jit(solution)/shard_map/ppermute | solution.py:193
  94.2 9.2 %collective-permute-start.20 = (bf16[256,512]{1,0:T(8,128)(2,1)S(1)}, bf16[256,512]{1,0:T(8,128)(2,1)S(1)}, u32[]{:S(2)}, u32[]{:S(2)}) collective-permute-start(bf16[256,512]{1,0:T(8,128)(2,1)S(1)} %slice.129), channel_id=1, source_target_pairs={{0,8},{4,12},{8,0},{12,4},{16,24},{20,28},{24,16},{28,20},{1,9},{5... | collective-permute-start | bytes 786440 | tf_op jit(solution)/shard_map/ppermute | solution.py:193
  96.1 12.5 %collective-permute-start.24 = (bf16[256,512]{1,0:T(8,128)(2,1)S(1)}, bf16[256,512]{1,0:T(8,128)(2,1)S(1)}, u32[]{:S(2)}, u32[]{:S(2)}) collective-permute-start(bf16[256,512]{1,0:T(8,128)(2,1)S(1)} %slice.128), channel_id=1, source_target_pairs={{0,8},{4,12},{8,0},{12,4},{16,24},{20,28},{24,16},{28,20},{1,9},{5... | collective-permute-start | bytes 786440 | tf_op jit(solution)/shard_map/ppermute | solution.py:193
  (9 other events, 92.2 us)
